TPU v7x, 128 devices: a whole 4x4x4 slice. The times are simulated.
128 devices in a mesh: row: 16 (over x, y), col: 8 (over z, core).
Axes of the slice: x: 4, y: 4, z: 4, core: 2. Of those that a mesh axis runs over, the one named last changes fastest.
Arguments:
- orbitals: bfloat16 [131072, 512], P(('row', 'col')), may hold values from -6 to 6
- coulomb: bfloat16 [32768, 32768], P('row', 'col'), may hold values from -0.0014648438 to 0.0014648438
- interp: bfloat16 [131072, 1024], P(('row', 'col')), may hold values from -0.1875 to 0.1875
- box_counts: int32 [128], replicated, may hold values from 1 to 768, 32768 in all
- owner_map: int32 [32768], replicated, may hold values from 0 to 32767, as said below
- grid_rows: int32 [128, 1024], P(('row', 'col')), may hold values from 0 to 1023, each once within a row
- listed: int32 [128, 1024], P(('row', 'col')), may hold values from 0 to 255
Outputs:
- exchange_action: float32 [131072, 512], P(('row', 'col'))
Inputs may be any that keep to these rules, and one draw needn't show every extreme that they name: `box_counts`: the counts sum to 32768; the largest is exactly 768. `owner_map`: A permutation of the 32768 positions; a point's owner is position // 256. No box holds more than 6 points of one owner, and the box with 768 points holds exactly 6 of some owner. `grid_rows`: each row is a permutation.
All inputs are finite; a program needn't handle non-finite values.
Results may differ from a plain program's by a relative error of at most 0.012.
Values may be sent and summed in bfloat16 or wider, within the bound.
A program may use at most 128 MiB of HBM per device.

v0:
```python
import jax
import jax.numpy as jnp
from jax import lax
from jax.sharding import PartitionSpec as P

NORB = 512
LIST = 1024
OWN = 256
SLOTS = 768


def copy_for_each(x, axis):
    copies = jnp.broadcast_to(x, (lax.axis_size(axis), *x.shape))
    return lax.all_to_all(copies, axis, split_axis=0, concat_axis=0, tiled=True)


def in_order(parts, dim):
    parts = jnp.moveaxis(parts, 0, dim)
    dims = parts.shape
    return parts.reshape(*dims[:dim], dims[dim] * dims[dim + 1], *dims[dim + 2 :])


def gather_directly(x, axis, dim):
    parts = copy_for_each(x, axis)
    return in_order(parts, dim)


def add_block(shard_rows, left_rows, kernel_tile):
    pair_tile = jnp.einsum(
        "ak,bk->ab", left_rows, shard_rows, preferred_element_type=jnp.float32
    ).astype(jnp.bfloat16)
    weighted = (pair_tile.astype(jnp.float32) * kernel_tile.astype(jnp.float32)).astype(
        jnp.bfloat16
    )
    return jnp.dot(weighted, shard_rows, preferred_element_type=jnp.float32)


def shards(orbitals, coulomb, interp, box_counts, owner_map, grid_rows, listed):
    row_count = lax.axis_size("row")
    col_count = lax.axis_size("col")
    box_total = row_count * col_count
    point_total = OWN * box_total
    capacity = (SLOTS + box_total - 1) // box_total
    per_owner = LIST // box_total
    my_box = lax.axis_index("row") * col_count + lax.axis_index("col")
    box_ids = jnp.arange(box_total, dtype=jnp.int32)
    first_point = jnp.sum(jnp.where(box_ids < my_box, box_counts, 0))
    my_count = jnp.sum(jnp.where(box_ids == my_box, box_counts, 0))
    slot_ids = jnp.arange(SLOTS, dtype=jnp.int32)
    is_live = slot_ids < my_count
    listing = jnp.minimum(first_point + slot_ids, point_total - 1)
    owner_ids = owner_map[listing] // OWN
    matches = (
        (owner_ids[:, None] == owner_ids[None, :])
        & is_live[None, :]
        & (slot_ids[None, :] < slot_ids[:, None])
    )
    pair_rank = jnp.sum(matches.astype(jnp.int32), axis=1)
    target = jnp.where(is_live, owner_ids * capacity + pair_rank, box_total * capacity)
    dest_slots = jnp.arange(box_total * capacity, dtype=jnp.int32)
    hits = target[None, :] == dest_slots[:, None]
    source_slot = jnp.sum(jnp.where(hits, slot_ids[None, :], 0), axis=1)
    filled = jnp.any(hits, axis=1)
    picked = orbitals[grid_rows[0, source_slot]]
    outgoing = jnp.where(filled[:, None], picked, jnp.zeros_like(picked))
    received = lax.all_to_all(
        outgoing.reshape(box_total, capacity, NORB),
        ("row", "col"),
        split_axis=0,
        concat_axis=0,
        tiled=True,
    )
    received = received.reshape(box_total * capacity, NORB)
    wanted_pos = my_box * OWN + jnp.arange(OWN, dtype=jnp.int32)
    all_listing = jnp.arange(point_total, dtype=jnp.int32)
    my_points = jnp.sum(
        jnp.where(owner_map[None, :] == wanted_pos[:, None], all_listing[None, :], 0), axis=1
    )
    box_ends = jnp.cumsum(box_counts)
    source = jnp.sum((my_points[:, None] >= box_ends[None, :]).astype(jnp.int32), axis=1)
    earlier = (source[:, None] == source[None, :]) & (my_points[None, :] < my_points[:, None])
    source_rank = jnp.sum(earlier.astype(jnp.int32), axis=1)
    owned_rows = received[source * capacity + source_rank]
    left_rows = gather_directly(owned_rows, "col", 0)
    partial_sums = add_block(
        lax.all_gather(owned_rows, "row", axis=0, tiled=True), left_rows, coulomb
    )
    owned_result = lax.psum_scatter(partial_sums, "col", scatter_dimension=0, tiled=True).astype(
        jnp.bfloat16
    )
    wanted = listed[0].reshape(box_total, per_owner)
    fetched = lax.all_to_all(
        owned_result[
            lax.all_to_all(wanted, ("row", "col"), split_axis=0, concat_axis=0, tiled=True)
        ],
        ("row", "col"),
        split_axis=0,
        concat_axis=0,
        tiled=True,
    )
    chosen_rows = fetched.reshape(LIST, NORB)
    return -jnp.dot(interp, chosen_rows, preferred_element_type=jnp.float32)


def solution(mesh):
    return jax.shard_map(
        shards,
        mesh=mesh,
        in_specs=(
            P(("row", "col"), None),
            P("row", "col"),
            P(("row", "col"), None),
            P(),
            P(),
            P(("row", "col"), None),
            P(("row", "col"), None),
        ),
        out_specs=P(("row", "col"), None),
        check_vma=False,
    )
```

profile of v0, /device:TPU:25, one launch (start us, length us, event | category | flops | bytes accessed | tf_op | source)
XLA Modules:
  0.0 214.2 jit_solution(2038270782259860773)
XLA Ops:
  6.5 1.5 fusion.12
  8.1 0.7 fusion.7
  8.8 4.7 %gather_fusion = s32[768]{0:T(1024)S(1)} fusion(s32[32768]{0:T(1024)} %param.11, s32[1024]{0:T(1024)S(1)} %pad_clamp_fusion.2), kind=kCustom, calls=%fused_computation | custom fusion | bytes 9216 | tf_op jit(solution)/shard_map/gather | solution.py:52
  13.5 0.7 iota_compare_fusion.2
  16.0 4.7 %gather_fusion.1 = s32[768]{0:T(1024)S(1)} fusion(s32[1,1024]{1,0:T(1,128)S(1)} %copy-done.1, s32[768]{0:T(1024)S(1)} %fusion.11), kind=kCustom, calls=%fused_computation.1 | custom fusion | bytes 12288 | tf_op jit(solution)/shard_map/gather | solution.py:64
  20.7 3.3 %gather_fusion.2 = bf16[768,512]{1,0:T(8,128)(2,1)} fusion(bf16[1024,512]{1,0:T(8,128)(2,1)S(1)} %copy-done.3, s32[1024]{0:T(1024)S(1)} %pad_clamp_fusion.1), kind=kCustom, calls=%fused_computation.2 | custom fusion | bytes 1575936 | tf_op jit(solution)/shard_map/gather | solution.py:64
  24.1 1.3 gather.23
  25.6 1.2 broadcast_select_fusion
  26.8 11.0 %all-to-all-start = ((bf16[128,6,512]{2,1,0:T(8,128)(2,1)}), bf16[128,6,512]{2,1,0:T(8,128)(2,1)}, u32[]{:S(2)}, u32[]{:S(2)}) async-start(bf16[128,6,512]{2,1,0:T(8,128)(2,1)} %broadcast_select_fusion), calls=%async_computation | async-start | bytes 2097152 | tf_op jit(solution)/shard_map/all_to_all | solution.py:66
  37.9 4.6 %select_reduce_fusion = s32[256]{0:T(256)S(1)} fusion(s32[32768]{0:T(1024)S(1)} %copy-done.2, s32[256]{0:T(256)S(1)} %iota_add_fusion), kind=kLoop, calls=%fused_computation.6 | loop fusion | flops 25165568 | bytes 133120 | tf_op jit(solution)/shard_map/reduce_sum | solution.py:76
  43.4 11.6 %all-to-all-done = bf16[128,6,512]{2,1,0:T(8,128)(2,1)} async-done(((bf16[128,6,512]{2,1,0:T(8,128)(2,1)}), bf16[128,6,512]{2,1,0:T(8,128)(2,1)}, u32[]{:S(2)}, u32[]{:S(2)}) %all-to-all-start) | async-done | bytes 786464 | tf_op jit(solution)/shard_map/all_to_all | solution.py:66
  55.0 1.4 reshape.199
  56.4 1.9 gather_fusion.3
  58.3 1.1 broadcast_in_dim.79
  59.4 30.2 %all_to_all.27 = bf16[8,256,512]{2,1,0:T(8,128)(2,1)} all-to-all(bf16[8,256,512]{2,1,0:T(8,128)(2,1)S(1)} %broadcast_in_dim.79), channel_id=1, replica_groups=mesh['row'=16,'col'=8] {'col'}, dimensions={0} | all-to-all | bytes 4194304 | tf_op jit(solution)/shard_map/all_to_all | solution.py:14
  89.6 17.9 %all-gather.3.cloned.1.call-done = bf16[4096,512]{1,0:T(8,128)(2,1)} async-done(((bf16[256,512]{1,0:T(8,128)(2,1)}), bf16[4096,512]{1,0:T(8,128)(2,1)}) %all-gather.3.cloned.1.call-update) | async-done | bytes 4194320 | tf_op jit(solution)/shard_map/all_gather | solution.py:86
  107.5 26.1 %fusion = f32[2048,512]{1,0:T(8,128)} fusion(bf16[4096,512]{1,0:T(8,128)(2,1)} %all-gather.3.cloned.1.call-done, bf16[2048,4096]{1,0:T(8,128)(2,1)} %param.8, bf16[2048,512]{1,0:T(8,128)(2,1)} %bitcast.27), kind=kOutput, calls=%fused_computation.7 | convolution fusion | flops 17213423616 | bytes 27262976 | tf_op jit(solution)/shard_map/dot_general | solution.py:35
  135.1 15.9 %all_to_all.28 = s32[128,1,8]{2,1,0:T(1,128)S(1)} all-to-all(s32[128,1,8]{2,1,0:T(1,128)S(1)} %bitcast.28), channel_id=1, replica_groups=mesh['row'=16,'col'=8] {'row','col'}, dimensions={0} | all-to-all | bytes 8192 | tf_op jit(solution)/shard_map/all_to_all | solution.py:94
  151.1 18.3 %reduce-scatter.2.cloned.1.call-done = f32[256,512]{1,0:T(8,128)} async-done(((f32[2048,512]{1,0:T(8,128)}), f32[256,512]{1,0:T(8,128)}) %reduce-scatter.2.cloned.1.call-update) | async-done | bytes 524304 | tf_op jit(solution)/shard_map/reduce_scatter | solution.py:88
  169.4 1.1 convert_element_type.31
  170.4 4.0 %gather_fusion.4 = bf16[1024,512]{1,0:T(8,128)(2,1)S(1)} fusion(bf16[256,512]{1,0:T(8,128)(2,1)S(1)} %convert_element_type.31, s32[1024]{0:T(1024)S(1)} %broadcast_clamp_fusion), kind=kCustom, calls=%fused_computation.4 | custom fusion | bytes 2101248 | tf_op jit(solution)/shard_map/gather | solution.py:93
  174.4 27.4 %all_to_all.29 = bf16[128,8,512]{2,1,0:T(8,128)(2,1)S(1)} all-to-all(bf16[128,8,512]{2,1,0:T(8,128)(2,1)S(1)} %bitcast.26), channel_id=1, replica_groups=mesh['row'=16,'col'=8] {'row','col'}, dimensions={0} | all-to-all | bytes 2097152 | tf_op jit(solution)/shard_map/all_to_all | solution.py:92
  201.8 2.7 %negate_bitcast_fusion = f32[1024,512]{0,1:T(8,128)} fusion(bf16[1024,1024]{1,0:T(8,128)(2,1)S(1)} %copy-done, bf16[128,8,512]{2,1,0:T(8,128)(2,1)S(1)} %all_to_all.29), kind=kOutput, calls=%fused_computation.15 | convolution fusion | flops 1074266112 | bytes 5242880 | tf_op jit(solution)/shard_map/dot_general | solution.py:102
  204.5 2.9 %copy.17 = f32[1024,512]{1,0:T(8,128)} copy(f32[1024,512]{0,1:T(8,128)} %negate_bitcast_fusion) | data formatting | bytes 4194304 | tf_op jit(solution)/shard_map/neg | solution.py:102
  (41 shorter events, 4.4 us)
Async XLA Ops:
  6.5 195.3 %copy-start = (bf16[1024,1024]{1,0:T(8,128)(2,1)S(1)}, bf16[1024,1024]{1,0:T(8,128)(2,1)}, u32[]{:S(2)}) copy-start(bf16[1024,1024]{1,0:T(8,128)(2,1)} %param.9) | copy-start | bytes 6291460
  6.5 9.5 %copy-start.1 = (s32[1,1024]{1,0:T(1,128)S(1)}, s32[1,1024]{1,0:T(1,128)}, u32[]{:S(2)}) copy-start(s32[1,1024]{1,0:T(1,128)} %param.12) | copy-start | bytes 12292
  13.5 7.3 %copy-start.3 = (bf16[1024,512]{1,0:T(8,128)(2,1)S(1)}, bf16[1024,512]{1,0:T(8,128)(2,1)}, u32[]{:S(2)}) copy-start(bf16[1024,512]{1,0:T(8,128)(2,1)} %param.7) | copy-start | bytes 3145732
  25.4 12.5 %copy-start.2 = (s32[32768]{0:T(1024)S(1)}, s32[32768]{0:T(1024)}, u32[]{:S(2)}) copy-start(s32[32768]{0:T(1024)} %param.11) | copy-start | bytes 393220
  25.4 17.1 %copy-start.5 = (s32[128]{0:T(128)S(1)}, s32[128]{0:T(128)}, u32[]{:S(2)}) copy-start(s32[128]{0:T(128)} %param.10) | copy-start | bytes 1540
  26.8 28.2 %all-to-all-start = ((bf16[128,6,512]{2,1,0:T(8,128)(2,1)}), bf16[128,6,512]{2,1,0:T(8,128)(2,1)}, u32[]{:S(2)}, u32[]{:S(2)}) async-start(bf16[128,6,512]{2,1,0:T(8,128)(2,1)} %broadcast_select_fusion), calls=%async_computation | async-start | bytes 2097152 | tf_op jit(solution)/shard_map/all_to_all | solution.py:66
  37.8 69.7 %all-gather.3.cloned.1.call-start = ((), (), s32[]{:S(2)}) async-start(), calls=%async_computation.6 | async-start | bytes 4456448 | tf_op jit(solution)/shard_map/all_gather | solution.py:86
  58.2 111.1 %reduce-scatter.2.cloned.1.call-start = ((), (), s32[]{:S(2)}) async-start(), calls=%async_computation.5 | async-start | bytes 4718592 | tf_op jit(solution)/shard_map/reduce_scatter | solution.py:88
  133.6 0.7 copy-start.4
Sparse Core Ops, SparseCore 0:
  58.4 49.1 all-gather.2
  133.8 35.5 reduce-scatter.1
where the time goes:
time: 217 us; the launch traced here: 214 us
  blocking collectives  73.5 us (34%)
  waiting for transfers between devices  47.8 us (22%)
  matrix products  28.8 us (13%)
  local copies, waits for them, and re-layouts  26.3 us (12%)
  between operations  13.7 us (6%)
  other arithmetic  13 us (6%)
  starting transfers between devices  11.1 us (5%)
    all_to_all x1, blocking collectives, copy_for_each(): return lax.all_to_all(copies, axis, split_axis=0, concat_axis=0, tiled=True)  30.2 us
    all_to_all x1, blocking collectives, shards(): lax.all_to_all(owned_result[lax.all_to_all(wanted, ('row', 'col'), split_...  27.4 us
    dot_general x1, matrix products, add_block(): return jnp.dot(weighted, shard_rows, preferred_element_type=jnp.float32)  26.1 us
    reduce_scatter x1, waiting for transfers between devices, shards(): lax.psum_scatter(partial_sums, 'col', scatter_dimension=0, tiled=True)  18.3 us
    all_gather x1, waiting for transfers between devices, shards(): lax.all_gather(owned_rows, 'row', axis=0, tiled=True)  17.9 us
    all_to_all x1, blocking collectives, shards(): lax.all_to_all(wanted, ('row', 'col'), split_axis=0, concat_axis=0, tiled...  15.9 us
    all_to_all x1, waiting for transfers between devices, shards(): lax.all_to_all(outgoing.reshape(box_total, capacity, NORB), ('row', 'col'...  11.6 us
    all_to_all x1, starting transfers between devices, shards(): lax.all_to_all(outgoing.reshape(box_total, capacity, NORB), ('row', 'col'...  11 us
  transfers between devices with their start and end apart: 3, of which 3 were waited for; matrix products, arithmetic and copies ran while one was open for 4% of the time, Pallas kernels for 0%

commit v1 on v0

v1 whole, which is shorter than its diff:
```python
import jax
import jax.numpy as jnp
from jax import lax
from jax.sharding import PartitionSpec as P

NORB = 512
LIST = 1024
OWN = 256
SLOTS = 768
BOTH = ("row", "col")
F32 = jnp.float32
BF16 = jnp.bfloat16


def exchange(chunks):
    return lax.all_to_all(chunks, BOTH, split_axis=0, concat_axis=0, tiled=True)


def pick(index, rows, count):
    one_hot = (index[:, None] == jnp.arange(count, dtype=jnp.int32)[None, :]).astype(BF16)
    return jnp.dot(one_hot, rows, preferred_element_type=F32).astype(BF16)


def add_block(shard_rows, left_rows, kernel_tile):
    pair_tile = jnp.einsum(
        "ak,bk->ab", left_rows, shard_rows, preferred_element_type=F32
    ).astype(BF16)
    weighted = (pair_tile.astype(F32) * kernel_tile.astype(F32)).astype(BF16)
    return jnp.dot(weighted, shard_rows, preferred_element_type=F32)


def outgoing_chunks(orbitals, box_counts, owner_map, grid_rows, listed, my_box, box_total, lanes):
    per_owner = LIST // box_total
    box_ids = jnp.arange(box_total, dtype=jnp.int32)
    first_point = jnp.sum(jnp.where(box_ids < my_box, box_counts, 0))
    my_count = jnp.sum(jnp.where(box_ids == my_box, box_counts, 0))
    slot_ids = jnp.arange(SLOTS, dtype=jnp.int32)
    is_live = slot_ids < my_count
    padded = jnp.concatenate([owner_map, jnp.zeros((SLOTS,), jnp.int32)])
    position = lax.dynamic_slice(padded, (first_point,), (SLOTS,))
    owner_ids = position // OWN
    local_ids = position - owner_ids * OWN
    matches = (
        (owner_ids[:, None] == owner_ids[None, :])
        & is_live[None, :]
        & (slot_ids[None, :] < slot_ids[:, None])
    )
    pair_rank = jnp.sum(matches.astype(jnp.int32), axis=1)
    target = jnp.where(is_live, owner_ids * lanes + pair_rank, -1)
    dest = jnp.arange(box_total * lanes, dtype=jnp.int32)
    hits = target[None, :] == dest[:, None]
    coded = (grid_rows[0, :SLOTS] + 1) * OWN + local_ids
    found = jnp.sum(jnp.where(hits, coded[None, :], 0), axis=1)
    grid = found // OWN - 1
    local = jnp.where(found > 0, found - (grid + 1) * OWN, -1)
    picked = pick(grid, orbitals, orbitals.shape[0]).reshape(box_total, lanes, NORB)
    meta = jnp.stack([listed[0].reshape(box_total, per_owner), local.reshape(box_total, lanes)], axis=1)
    meta = jnp.pad(meta.astype(BF16), ((0, 0), (lanes - 2, 0), (0, NORB - per_owner)))
    row_ids = jnp.arange(lanes)[None, :, None]
    return jnp.where(row_ids < lanes - 2, picked, meta)


def shards(orbitals, coulomb, interp, box_counts, owner_map, grid_rows, listed):
    box_total = lax.axis_size("row") * lax.axis_size("col")
    lanes = LIST // box_total
    my_box = lax.axis_index("row") * lax.axis_size("col") + lax.axis_index("col")
    received = exchange(
        outgoing_chunks(orbitals, box_counts, owner_map, grid_rows, listed, my_box, box_total, lanes)
    )
    wanted = received[:, lanes - 2, :lanes].astype(jnp.int32).reshape(-1)
    local = received[:, lanes - 1, :lanes].astype(jnp.int32).reshape(-1)
    place = (local[None, :] == jnp.arange(OWN, dtype=jnp.int32)[:, None]).astype(BF16)
    owned_rows = jnp.dot(
        place, received.reshape(box_total * lanes, NORB), preferred_element_type=F32
    ).astype(BF16)
    left_rows = lax.all_gather(owned_rows, "col", axis=0, tiled=True)
    column_rows = lax.all_gather(owned_rows, "row", axis=0, tiled=True)
    partial_sums = add_block(column_rows, left_rows, coulomb)
    owned_result = lax.psum_scatter(partial_sums, "col", scatter_dimension=0, tiled=True).astype(BF16)
    fetched = exchange(pick(wanted, owned_result, OWN).reshape(box_total, lanes, NORB))
    return -jnp.dot(interp, fetched.reshape(LIST, NORB), preferred_element_type=F32)


def solution(mesh):
    return jax.shard_map(
        shards,
        mesh=mesh,
        in_specs=(
            P(BOTH, None),
            P("row", "col"),
            P(BOTH, None),
            P(),
            P(),
            P(BOTH, None),
            P(BOTH, None),
        ),
        out_specs=P(BOTH, None),
        check_vma=False,
    )
```

time: 217 us -> 231 us (1.065)
  waiting for transfers between devices: 47.8 us -> 112 us
  local copies, waits for them, and re-layouts: 26.3 us -> 3.82 us
  blocking collectives: 73.5 us -> 55.5 us
  starting transfers between devices: 11.1 us -> 0.08 us
  other arithmetic: 13 us -> 6.9 us
  matrix products: 28.8 us -> 34 us
    all_gather x1 -> x2, waiting for transfers between devices: 17.9 us -> 76.4 us  [the longest x1 53.5 us: shards(): column_rows = lax.all_gather(owned_rows, 'row', axis=0, tiled=True)]
    gather x6 -> x0, local copies, waits for them, and re-layouts: 19.8 us -> none  [the longest x3 9.33 us: shards(): picked = orbitals[grid_rows[0, source_slot]]]
    all_to_all x3 -> x2, blocking collectives: 73.5 us -> 55.5 us  [exchange(): return lax.all_to_all(chunks, BOTH, split_axis=0, concat_axis=0, tiled=True)]
    reduce_scatter x1, waiting for transfers between devices: 18.3 us -> 35 us  [shards(): lax.psum_scatter(partial_sums, 'col', scatter_dimension=0, tiled=True)]
    all_to_all x1 -> x0, waiting for transfers between devices: 11.6 us -> none  [shards(): lax.all_to_all(outgoing.reshape(box_total, capacity, NORB), ('row', 'col'...]
    all_to_all x1 -> x0, starting transfers between devices: 11 us -> none  [shards(): lax.all_to_all(outgoing.reshape(box_total, capacity, NORB), ('row', 'col'...]
    dot_general x2 -> x5, matrix products: 28.8 us -> 34 us  [the longest x1 26.1 us: add_block(): return jnp.dot(weighted, shard_rows, preferred_element_type=F32)]
    reduce_sum x6 -> x3, other arithmetic: 7.29 us -> 2.19 us  [the longest x1 1.38 us: outgoing_chunks(): my_count = jnp.sum(jnp.where(box_ids == my_box, box_counts, 0))]
  transfers between devices with their start and end apart: 3 -> 3, of which waited for: 3 -> 3; matrix products, arithmetic and copies ran while one was open for 4% -> 0% of each run, Pallas kernels for 0% -> 0%
where the time goes in v1:
time: 231 us; the launch traced here: 228 us
  waiting for transfers between devices  112 us (48%)
  blocking collectives  55.5 us (24%)
  matrix products  34 us (15%)
  between operations  15.3 us (7%)
  other arithmetic  6.9 us (3%)
  local copies, waits for them, and re-layouts  3.82 us (2%)
    all_to_all x2, blocking collectives, exchange(): return lax.all_to_all(chunks, BOTH, split_axis=0, concat_axis=0, tiled=True)  55.5 us
    all_gather x1, waiting for transfers between devices, shards(): column_rows = lax.all_gather(owned_rows, 'row', axis=0, tiled=True)  53.5 us
    reduce_scatter x1, waiting for transfers between devices, shards(): lax.psum_scatter(partial_sums, 'col', scatter_dimension=0, tiled=True)  35 us
    dot_general x1, matrix products, add_block(): return jnp.dot(weighted, shard_rows, preferred_element_type=F32)  26.1 us
    all_gather x1, waiting for transfers between devices, shards(): left_rows = lax.all_gather(owned_rows, 'col', axis=0, tiled=True)  22.9 us
  transfers between devices with their start and end apart: 3, of which 3 were waited for; matrix products, arithmetic and copies ran while one was open for 0% of the time, Pallas kernels for 0%

profile of v1, /device:TPU:25, one launch (start us, length us, event | category | flops | bytes accessed | tf_op | source)
XLA Modules:
  0.0 227.6 jit_solution(10312394453121893016)
XLA Ops:
  6.5 0.8 multiply_reduce_fusion
  7.4 1.4 fusion.33
  10.2 0.7 iota_compare_fusion.14
  11.5 0.9 subtract_add_fusion
  12.4 0.4 convert_reduce_fusion
  12.8 0.7 add_select_fusion.3
  13.4 0.4 select_reduce_fusion
  14.0 0.7 convert_reduce_fusion.1
  14.7 0.1 stack_reshape_squeeze.4
  14.8 2.5 %fusion.12 = bf16[128,8,512]{2,1,0:T(8,128)(2,1)S(1)} fusion(bf16[1024,512]{1,0:T(8,128)(2,1)} %param.7, s32[1024]{0:T(1024)S(1)} %fusion.30), kind=kOutput, calls=%fused_computation.22 | convolution fusion | flops 1075314688 | bytes 2101248 | tf_op jit(solution)/shard_map/dot_general | solution.py:21
  17.4 0.4 fusion.14
  17.8 0.6 copy.20
  18.4 27.9 %all_to_all.10 = bf16[128,8,512]{2,1,0:T(8,128)(2,1)S(1)} all-to-all(bf16[128,8,512]{2,1,0:T(8,128)(2,1)S(1)} %copy.20), channel_id=1, replica_groups=mesh['row'=16,'col'=8] {'row','col'}, dimensions={0} | all-to-all | bytes 2097152 | tf_op jit(solution)/shard_map/all_to_all | solution.py:16
  46.3 0.5 fusion.25
  46.9 1.2 convolution_convert_fusion.1
  48.1 0.7 all-gather.5.cloned.1.call-update
  48.8 22.9 %all-gather.3.cloned.1.call-done = bf16[2048,512]{1,0:T(8,128)(2,1)} async-done(((bf16[256,512]{1,0:T(8,128)(2,1)}), bf16[2048,512]{1,0:T(8,128)(2,1)}) %all-gather.3.cloned.1.call-update) | async-done | bytes 2097168 | tf_op jit(solution)/shard_map/all_gather | solution.py:76
  71.8 53.5 %all-gather.5.cloned.1.call-done = bf16[4096,512]{1,0:T(8,128)(2,1)} async-done(((bf16[256,512]{1,0:T(8,128)(2,1)}), bf16[4096,512]{1,0:T(8,128)(2,1)}) %all-gather.5.cloned.1.call-update) | async-done | bytes 4194320 | tf_op jit(solution)/shard_map/all_gather | solution.py:77
  125.2 26.1 %fusion = f32[2048,512]{1,0:T(8,128)} fusion(bf16[4096,512]{1,0:T(8,128)(2,1)} %all-gather.5.cloned.1.call-done, bf16[2048,4096]{1,0:T(8,128)(2,1)} %param.8, bf16[2048,512]{1,0:T(8,128)(2,1)} %all-gather.3.cloned.1.call-done), kind=kOutput, calls=%fused_computation.1 | convolution fusion | flops 17213423616 | bytes 27262976 | tf_op jit(solution)/shard_map/dot_general | solution.py:29
  151.5 35.0 %reduce-scatter.2.cloned.1.call-done = f32[256,512]{1,0:T(8,128)} async-done(((f32[2048,512]{1,0:T(8,128)}), f32[256,512]{1,0:T(8,128)}) %reduce-scatter.2.cloned.1.call-update) | async-done | bytes 524304 | tf_op jit(solution)/shard_map/reduce_scatter | solution.py:79
  186.4 1.5 fusion.11
  188.0 27.6 %all_to_all.11 = bf16[128,8,512]{2,1,0:T(8,128)(2,1)S(1)} all-to-all(bf16[128,8,512]{2,1,0:T(8,128)(2,1)S(1)} %fusion.11), channel_id=1, replica_groups=mesh['row'=16,'col'=8] {'row','col'}, dimensions={0} | all-to-all | bytes 2097152 | tf_op jit(solution)/shard_map/all_to_all | solution.py:16
  215.5 2.7 %negate_bitcast_fusion = f32[1024,512]{0,1:T(8,128)} fusion(bf16[1024,1024]{1,0:T(8,128)(2,1)S(1)} %copy-done, bf16[128,8,512]{2,1,0:T(8,128)(2,1)S(1)} %all_to_all.11), kind=kOutput, calls=%fused_computation.15 | convolution fusion | flops 1074266112 | bytes 5242880 | tf_op jit(solution)/shard_map/dot_general | solution.py:81
  218.2 2.9 %copy.21 = f32[1024,512]{1,0:T(8,128)} copy(f32[1024,512]{0,1:T(8,128)} %negate_bitcast_fusion) | data formatting | bytes 4194304 | tf_op jit(solution)/shard_map/neg | solution.py:81
  (13 shorter events, 0.5 us)
Async XLA Ops:
  6.5 209.0 %copy-start = (bf16[1024,1024]{1,0:T(8,128)(2,1)S(1)}, bf16[1024,1024]{1,0:T(8,128)(2,1)}, u32[]{:S(2)}) copy-start(bf16[1024,1024]{1,0:T(8,128)(2,1)} %param.9) | copy-start | bytes 6291460
  6.5 65.2 %all-gather.3.cloned.1.call-start = ((), (), s32[]{:S(2)}) async-start(), calls=%async_computation.3 | async-start | bytes 2359296 | tf_op jit(solution)/shard_map/all_gather | solution.py:76
  48.0 77.2 %all-gather.5.cloned.1.call-start = ((), (), s32[]{:S(2)}) async-start(), calls=%async_computation.4 | async-start | bytes 4456448 | tf_op jit(solution)/shard_map/all_gather | solution.py:77
  48.8 137.6 %reduce-scatter.2.cloned.1.call-start = ((), (), s32[]{:S(2)}) async-start(), calls=%async_computation.5 | async-start | bytes 4718592 | tf_op jit(solution)/shard_map/reduce_scatter | solution.py:79
Sparse Core Ops, SparseCore 0:
  48.1 23.5 all-gather.2
  73.9 51.2 all-gather.4
  151.5 34.8 reduce-scatter.1

commit v2 on v1

--- a/solution.py
+++ b/solution.py
@@ -1,6 +1,8 @@
 import jax
 import jax.numpy as jnp
 from jax import lax
+from jax.experimental import pallas as pl
+from jax.experimental.pallas import tpu as pltpu
 from jax.sharding import PartitionSpec as P
 
 NORB = 512
@@ -12,8 +14,270 @@
 BF16 = jnp.bfloat16
 
 
-def exchange(chunks):
-    return lax.all_to_all(chunks, BOTH, split_axis=0, concat_axis=0, tiled=True)
+SIDE = 4
+MESH = pl.DeviceIdType.MESH
+
+
+def greet(partners):
+    barrier = pltpu.get_barrier_semaphore()
+    for partner in partners:
+        pl.semaphore_signal(barrier, inc=1, device_id=partner, device_id_type=MESH)
+    pl.semaphore_wait(barrier, len(partners))
+
+
+def exchange_kernel(rows, cols, src, dst, send_sem, recv_sem, own_sem):
+    me = lax.axis_index("row") * cols + lax.axis_index("col")
+    count = rows * cols
+    barrier = pltpu.get_barrier_semaphore()
+
+    def place(step):
+        other = lax.rem(me + step, count)
+        return other, (other // cols, lax.rem(other, cols))
+
+    def signal(step, carry):
+        pl.semaphore_signal(barrier, inc=1, device_id=place(step)[1], device_id_type=MESH)
+        return carry
+
+    lax.fori_loop(1, count, signal, 0)
+    own = pltpu.make_async_copy(src.at[me], dst.at[me], own_sem)
+    own.start()
+    pl.semaphore_wait(barrier, count - 1)
+
+    def send(step, carry):
+        other, device = place(step)
+        pltpu.make_async_remote_copy(
+            src_ref=src.at[other],
+            dst_ref=dst.at[me],
+            send_sem=send_sem,
+            recv_sem=recv_sem,
+            device_id=device,
+            device_id_type=MESH,
+        ).start()
+        return carry
+
+    lax.fori_loop(1, count, send, 0)
+    own.wait()
+    many = pl.ds(0, count - 1)
+    pltpu.make_async_copy(src.at[many], dst.at[many], send_sem).wait()
+    pltpu.make_async_copy(src.at[many], dst.at[many], recv_sem).wait()
+
+
+def exchange(chunks, collective_id):
+    return pl.pallas_call(
+        lambda *refs: exchange_kernel(lax.axis_size("row"), lax.axis_size("col"), *refs),
+        out_shape=jax.ShapeDtypeStruct(chunks.shape, chunks.dtype),
+        in_specs=[pl.BlockSpec(memory_space=pltpu.VMEM)],
+        out_specs=pl.BlockSpec(memory_space=pltpu.VMEM),
+        scratch_shapes=[pltpu.SemaphoreType.DMA] * 3,
+        compiler_params=pltpu.CompilerParams(collective_id=collective_id, has_side_effects=True),
+    )(chunks)
+
+
+def around(at):
+    return lax.rem(at + SIDE - 1, SIDE), lax.rem(at + 1, SIDE), lax.rem(at + 2, SIDE)
+
+
+def gather_kernel(own, buf, left, send_sem, recv_sem, own_sem):
+    row, col = lax.axis_index("row"), lax.axis_index("col")
+    x, y = row // SIDE, lax.rem(row, SIDE)
+    z, core = col // 2, lax.rem(col, 2)
+    (xm, xp, xf), (ym, yp, yf), (zm, zp, zf) = around(x), around(y), around(z)
+    on_x = ((xm * SIDE + y, col), (xp * SIDE + y, col))
+    on_y = ((x * SIDE + ym, col), (x * SIDE + yp, col))
+    on_z = ((row, zm * 2 + core), (row, zp * 2 + core))
+    mate = (row, z * 2 + 1 - core)
+    used, started = [0], []
+
+    def push(src, dst, device, landing):
+        index = used[0]
+        used[0] += 1
+        pair = send_sem.at[index], recv_sem.at[index]
+        copy = pltpu.make_async_remote_copy(src, dst, *pair, device_id=device, device_id_type=MESH)
+        copy.start()
+        started.append(copy)
+        return pltpu.make_async_remote_copy(landing, landing, *pair, device_id=device, device_id_type=MESH)
+
+    greet([*on_x, *on_y, *on_z, mate])
+    local = [
+        pltpu.make_async_copy(own, buf.at[x, y], own_sem.at[0]),
+        pltpu.make_async_copy(own, left.at[z, core], own_sem.at[1]),
+    ]
+    for copy in local:
+        copy.start()
+
+    def slot(half, first, second):
+        return buf.at[second, first, 0] if half == 0 else buf.at[first, second, 1]
+
+    first_at = ((ym, y, yp, yf), (xm, x, xp, xf))
+    second_at = ((xm, x, xp, xf), (ym, y, yp, yf))
+    first_to, second_to = (on_y, on_x), (on_x, on_y)
+
+    def second_send(half, first, src=None):
+        minus, at, plus, _ = second_at[half]
+        here = slot(half, first, at)
+        src = here if src is None else src
+        return (
+            push(src, here, second_to[half][1], slot(half, first, minus)),
+            push(src, here, second_to[half][0], slot(half, first, plus)),
+        )
+
+    def relay(ring, targets, where):
+        minus, _, plus, far = ring
+        one = push(where(minus).at[0], where(minus).at[0], targets[1], where(far).at[0])
+        two = push(where(plus).at[1], where(plus).at[1], targets[0], where(far).at[1])
+        return one, two
+
+    first_waits = []
+    for half in range(2):
+        minus, at, plus, _ = first_at[half]
+        here = slot(half, at, second_at[half][1])
+        first_waits.append((
+            push(own.at[half], here, first_to[half][1], slot(half, minus, second_at[half][1])),
+            push(own.at[half], here, first_to[half][0], slot(half, plus, second_at[half][1])),
+        ))
+    second_waits = [[(first_at[h][1], second_send(h, first_at[h][1], own.at[h]))] for h in range(2)]
+    z_waits = (
+        push(own, left.at[z, core], on_z[1], left.at[zm, core]),
+        push(own, left.at[z, core], on_z[0], left.at[zp, core]),
+    )
+    mate_waits = [push(own, left.at[z, core], mate, left.at[z, 1 - core])]
+    first_far = []
+    for half in range(2):
+        for wait in first_waits[half]:
+            wait.wait_recv()
+        at = second_at[half][1]
+        first_far.append(relay(first_at[half], first_to[half], lambda f, h=half, s=at: slot(h, f, s)))
+        for k in (0, 2):
+            second_waits[half].append((first_at[half][k], second_send(half, first_at[half][k])))
+    for wait in z_waits:
+        wait.wait_recv()
+    z_far = relay((zm, z, zp, zf), on_z, lambda at: left.at[at, core])
+    for at in (zm, zp):
+        mate_waits.append(push(left.at[at, core], left.at[at, core], mate, left.at[at, 1 - core]))
+    last = []
+
+    def second_relay(half, first, waits):
+        for wait in waits:
+            wait.wait_recv()
+        last.extend(relay(second_at[half], second_to[half], lambda s: slot(half, first, s)))
+
+    for half in range(2):
+        second_relay(half, *second_waits[half][0])
+    for half in range(2):
+        for wait in first_far[half]:
+            wait.wait_recv()
+        far = first_at[half][3]
+        second_waits[half].append((far, second_send(half, far)))
+    for wait in z_far:
+        wait.wait_recv()
+    mate_waits.append(push(left.at[zf, core], left.at[zf, core], mate, left.at[zf, 1 - core]))
+    for k in (1, 2, 3):
+        for half in range(2):
+            second_relay(half, *second_waits[half][k])
+    for wait in last + mate_waits:
+        wait.wait_recv()
+    for copy in started:
+        copy.wait_send()
+    for copy in local:
+        copy.wait()
+
+
+COPIES = 2 * (4 + 4 * 4) + 4 + 4
+
+
+def gather_rows(owned_rows):
+    rows, norb = owned_rows.shape
+    own = owned_rows.reshape(2, 2, rows // 4, norb)
+    vmem = pl.BlockSpec(memory_space=pltpu.VMEM)
+    buf, left = pl.pallas_call(
+        gather_kernel,
+        out_shape=(
+            jax.ShapeDtypeStruct((SIDE, SIDE, *own.shape), own.dtype),
+            jax.ShapeDtypeStruct((SIDE, 2, *own.shape), own.dtype),
+        ),
+        in_specs=[vmem],
+        out_specs=(vmem, vmem),
+        scratch_shapes=[
+            pltpu.SemaphoreType.DMA((COPIES,)),
+            pltpu.SemaphoreType.DMA((COPIES,)),
+            pltpu.SemaphoreType.DMA((2,)),
+        ],
+        compiler_params=pltpu.CompilerParams(collective_id=1, has_side_effects=True),
+    )(own)
+    return buf.reshape(-1, norb), left.reshape(-1, norb)
+
+
+STRIP = 32
+
+
+def scatter_kernel(src, out, inbox, stage, halves, blocks, send_sem, recv_sem):
+    row, col = lax.axis_index("row"), lax.axis_index("col")
+    z, core = col // 2, lax.rem(col, 2)
+    zm, zp, zf = around(z)
+    minus, plus = (row, zm * 2 + core), (row, zp * 2 + core)
+    mate = (row, z * 2 + 1 - core)
+    half = src.shape[2] // 2
+    greet([minus, plus, mate])
+
+    def push(index, src_ref, dst_ref, device):
+        copy = pltpu.make_async_remote_copy(
+            src_ref, dst_ref, send_sem.at[index], recv_sem.at[index], device_id=device, device_id_type=MESH
+        )
+        copy.start()
+        return copy
+
+    mates = [push(i, src.at[at, 1 - core], inbox.at[at], mate) for i, at in enumerate((zf, zp, zm, z))]
+
+    def add(at, start, size, write, *more):
+        @pl.loop(0, size // STRIP)
+        def _(i):
+            rows = pl.ds(pl.multiple_of(start + i * STRIP, STRIP), STRIP)
+            total = src[at, core, rows, :].astype(F32) + inbox[at, rows, :].astype(F32)
+            for ref, shift in more:
+                part = pl.ds(pl.multiple_of(start - shift + i * STRIP, STRIP), STRIP)
+                total += ref[part, :].astype(F32)
+            write[rows, :] = total.astype(BF16)
+
+    mates[0].wait_recv()
+    add(zf, 0, 2 * half, stage.at[0])
+    up = push(4, stage.at[0, pl.ds(0, half)], halves.at[0], plus)
+    down = push(5, stage.at[0, pl.ds(half, half)], halves.at[1], minus)
+    mates[1].wait_recv()
+    add(zp, half, half, stage.at[1])
+    mates[2].wait_recv()
+    add(zm, 0, half, stage.at[2])
+    up.wait_recv()
+    add(zp, 0, half, stage.at[1], (halves.at[0], 0))
+    up_block = push(6, stage.at[1], blocks.at[0], plus)
+    down.wait_recv()
+    add(zm, half, half, stage.at[2], (halves.at[1], half))
+    down_block = push(7, stage.at[2], blocks.at[1], minus)
+    mates[3].wait_recv()
+    up_block.wait_recv()
+    down_block.wait_recv()
+    add(z, 0, 2 * half, out, (blocks.at[0], 0), (blocks.at[1], 0))
+    for copy in (*mates, up, down, up_block, down_block):
+        copy.wait_send()
+
+
+def scatter_sums(partial_sums):
+    norb = partial_sums.shape[1]
+    vmem = pl.BlockSpec(memory_space=pltpu.VMEM)
+    return pl.pallas_call(
+        scatter_kernel,
+        out_shape=jax.ShapeDtypeStruct((OWN, norb), BF16),
+        in_specs=[vmem],
+        out_specs=vmem,
+        scratch_shapes=[
+            pltpu.VMEM((SIDE, OWN, norb), BF16),
+            pltpu.VMEM((3, OWN, norb), BF16),
+            pltpu.VMEM((2, OWN // 2, norb), BF16),
+            pltpu.VMEM((2, OWN, norb), BF16),
+            pltpu.SemaphoreType.DMA((8,)),
+            pltpu.SemaphoreType.DMA((8,)),
+        ],
+        compiler_params=pltpu.CompilerParams(collective_id=2, has_side_effects=True),
+    )(partial_sums.reshape(SIDE, 2, OWN, norb))
 
 
 def pick(index, rows, count):
@@ -65,7 +329,8 @@
     lanes = LIST // box_total
     my_box = lax.axis_index("row") * lax.axis_size("col") + lax.axis_index("col")
     received = exchange(
-        outgoing_chunks(orbitals, box_counts, owner_map, grid_rows, listed, my_box, box_total, lanes)
+        outgoing_chunks(orbitals, box_counts, owner_map, grid_rows, listed, my_box, box_total, lanes),
+        0,
     )
     wanted = received[:, lanes - 2, :lanes].astype(jnp.int32).reshape(-1)
     local = received[:, lanes - 1, :lanes].astype(jnp.int32).reshape(-1)
@@ -73,11 +338,10 @@
     owned_rows = jnp.dot(
         place, received.reshape(box_total * lanes, NORB), preferred_element_type=F32
     ).astype(BF16)
-    left_rows = lax.all_gather(owned_rows, "col", axis=0, tiled=True)
-    column_rows = lax.all_gather(owned_rows, "row", axis=0, tiled=True)
-    partial_sums = add_block(column_rows, left_rows, coulomb)
-    owned_result = lax.psum_scatter(partial_sums, "col", scatter_dimension=0, tiled=True).astype(BF16)
-    fetched = exchange(pick(wanted, owned_result, OWN).reshape(box_total, lanes, NORB))
+    column_rows, left_rows = gather_rows(owned_rows)
+    partial_sums = add_block(column_rows, left_rows, coulomb).astype(BF16)
+    owned_result = scatter_sums(partial_sums)
+    fetched = exchange(pick(wanted, owned_result, OWN).reshape(box_total, lanes, NORB), 3)
     return -jnp.dot(interp, fetched.reshape(LIST, NORB), preferred_element_type=F32)
 
 

time: 231 us -> 158 us (0.68); the launches traced: 228 us -> 158 us
  waiting for transfers between devices: 112 us -> 0 us
  Pallas kernels: 0 us -> 106 us
  blocking collectives: 55.5 us -> 0 us
  between operations: 15.3 us -> 2.17 us
  matrix products: 34 us -> 38.2 us
    pallas_call x0 -> x4, Pallas kernels: none -> 106 us  [the longest x2 57 us: exchange(): pl.pallas_call(lambda *refs: exchange_kernel(lax.axis_size('row'), lax.ax...]
    all_gather x2 -> x0, waiting for transfers between devices: 76.4 us -> none  [the longest x1 53.5 us: shards(): column_rows = lax.all_gather(owned_rows, 'row', axis=0, tiled=True)]
    all_to_all x2 -> x0, blocking collectives: 55.5 us -> none  [exchange(): return lax.all_to_all(chunks, BOTH, split_axis=0, concat_axis=0, tiled=True)]
    reduce_scatter x1 -> x0, waiting for transfers between devices: 35 us -> none  [shards(): lax.psum_scatter(partial_sums, 'col', scatter_dimension=0, tiled=True)]
  transfers between devices with their start and end apart: 3 -> 0, of which waited for: 3 -> 0; matrix products, arithmetic and copies ran while one was open for 0% -> 0% of each run, Pallas kernels for 0% -> 0%
where the time goes in v2:
time: 158 us
  Pallas kernels  106 us (67%)
  matrix products  38.2 us (24%)
  other arithmetic  7.86 us (5%)
  local copies, waits for them, and re-layouts  3.26 us (2%)
  between operations  2.17 us (1%)
    pallas_call x2, Pallas kernels, exchange(): pl.pallas_call(lambda *refs: exchange_kernel(lax.axis_size('row'), lax.ax...  57 us
    pallas_call x1, Pallas kernels, gather_rows(): pl.pallas_call(gather_kernel, out_shape=(jax.ShapeDtypeStruct((SIDE, SIDE...  29.4 us
    dot_general x1, matrix products, add_block(): return jnp.dot(weighted, shard_rows, preferred_element_type=F32)  25.9 us
    pallas_call x1, Pallas kernels, scatter_sums(): pl.pallas_call(scatter_kernel, out_shape=jax.ShapeDtypeStruct((OWN, norb)...  19.9 us
    dot_general x2, matrix products, pick(): return jnp.dot(one_hot, rows, preferred_element_type=F32).astype(BF16)  6.09 us
    dot_general x1, matrix products, shards(): jnp.dot(interp, fetched.reshape(LIST, NORB), preferred_element_type=F32)  3.87 us

profile of v2, /device:TPU:25, one launch (start us, length us, event | category | flops | bytes accessed | tf_op | source)
XLA Modules:
  0.0 157.8 jit_solution(104974203544293583)
XLA Ops:
  0.0 1.5 fusion.26
  3.6 0.7 iota_compare_fusion.16
  4.3 0.7 convert_reduce_fusion.3
  5.0 0.7 multiply_reduce_fusion
  5.7 0.9 subtract_add_fusion
  6.5 0.4 convert_reduce_fusion
  7.0 0.7 add_select_fusion.2
  7.6 0.4 select_reduce_fusion
  8.0 0.1 reduce_sum.42
  8.1 0.4 fusion.20
  8.5 0.1 stack_reshape_squeeze.5
  8.6 3.7 %fusion.14.refs_0_ = bf16[128,8,512]{2,1,0:T(8,128)(2,1)} fusion(bf16[1024,512]{1,0:T(8,128)(2,1)} %param.7, s32[1024]{0:T(1024)S(1)} %fusion.23, bf16[128,1,8]{2,1,0:T(2,128)(2,1)S(1)} %fusion.20, bf16[128,1,8]{2,1,0:T(2,128)(2,1)S(1)} %stack_reshape_squeeze.5, pred[8]{0:T(512)(128)(4,1)S(1)} %iota_compare_fusion.17), kind=kOutput, calls=%fused_computation.24 | convolution fusion | flops 1081606144 | bytes 2105352 | tf_op jit(solution)/shard_map/dot_general | solution.py:285
  12.3 29.2 %shard_map.73 = bf16[128,8,512]{2,1,0:T(8,128)(2,1)} custom-call(bf16[128,8,512]{2,1,0:T(8,128)(2,1)} %fusion.14.refs_0_), custom_call_target="tpu_custom_call" | custom-call | tf_op jit(solution)/shard_map/pallas_call | solution.py:66
  41.5 1.6 convert_reduce_fusion.2
  43.1 0.1 reshape.176
  43.2 0.1 reshape.177
  43.3 2.4 %convolution_convert_fusion.1 = bf16[256,512]{1,0:T(8,128)(2,1)} fusion(bf16[128,8,512]{2,1,0:T(8,128)(2,1)} %shard_map.73, s32[1024]{0:T(1024)S(1)} %reshape.177), kind=kOutput, calls=%fused_computation.25 | convolution fusion | flops 268828672 | bytes 1314816 | tf_op jit(solution)/shard_map/dot_general | solution.py:338
  45.6 29.4 %shard_map.74 = (bf16[4,4,2,2,64,512]{5,4,3,2,1,0:T(8,128)(2,1)}, bf16[4,2,2,2,64,512]{5,4,3,2,1,0:T(8,128)(2,1)}) custom-call(bf16[2,2,64,512]{3,2,1,0:T(8,128)(2,1)} %bitcast.39), custom_call_target="tpu_custom_call" | custom-call | tf_op jit(solution)/shard_map/pallas_call | solution.py:192
  75.0 25.9 %fusion.3 = bf16[2048,512]{1,0:T(8,128)(2,1)} fusion(bf16[4096,512]{1,0:T(8,128)(2,1)} %bitcast.41, bf16[2048,4096]{1,0:T(8,128)(2,1)} %param.8, bf16[2048,512]{1,0:T(8,128)(2,1)} %bitcast.42), kind=kOutput, calls=%fused_computation.7 | convolution fusion | flops 17214472192 | bytes 25165824 | tf_op jit(solution)/shard_map/dot_general | solution.py:293
  100.9 19.9 %shard_map.75 = bf16[256,512]{1,0:T(8,128)(2,1)} custom-call(bf16[4,2,256,512]{3,2,1,0:T(8,128)(2,1)} %bitcast.38), custom_call_target="tpu_custom_call" | custom-call | tf_op jit(solution)/shard_map/pallas_call | solution.py:266
  120.8 2.4 %fusion.12.refs_0_ = bf16[128,8,512]{2,1,0:T(8,128)(2,1)} fusion(bf16[256,512]{1,0:T(8,128)(2,1)} %shard_map.75, s32[1024]{0:T(1024)S(1)} %reshape.176), kind=kOutput, calls=%fused_computation.22 | convolution fusion | flops 269221888 | bytes 1314816 | tf_op jit(solution)/shard_map/dot_general | solution.py:285
  123.3 27.8 %shard_map.76 = bf16[128,8,512]{2,1,0:T(8,128)(2,1)} custom-call(bf16[128,8,512]{2,1,0:T(8,128)(2,1)} %fusion.12.refs_0_), custom_call_target="tpu_custom_call" | custom-call | tf_op jit(solution)/shard_map/pallas_call | solution.py:66
  151.0 3.9 %negate_bitcast_fusion = f32[1024,512]{0,1:T(8,128)} fusion(bf16[1024,1024]{1,0:T(8,128)(2,1)S(1)} %copy-done, bf16[128,8,512]{2,1,0:T(8,128)(2,1)} %shard_map.76), kind=kOutput, calls=%fused_computation.16 | convolution fusion | flops 1074266112 | bytes 5242880 | tf_op jit(solution)/shard_map/dot_general | solution.py:345
  154.9 2.9 %copy.28 = f32[1024,512]{1,0:T(8,128)} copy(f32[1024,512]{0,1:T(8,128)} %negate_bitcast_fusion) | data formatting | bytes 4194304 | tf_op jit(solution)/shard_map/neg | solution.py:345
  (4 shorter events, 0.0 us)
Async XLA Ops:
  0.0 151.0 %copy-start = (bf16[1024,1024]{1,0:T(8,128)(2,1)S(1)}, bf16[1024,1024]{1,0:T(8,128)(2,1)}, u32[]{:S(2)}) copy-start(bf16[1024,1024]{1,0:T(8,128)(2,1)} %param.9) | copy-start | bytes 6291460

commit v3 on v2

--- a/solution.py
+++ b/solution.py
@@ -77,7 +77,7 @@
     return lax.rem(at + SIDE - 1, SIDE), lax.rem(at + 1, SIDE), lax.rem(at + 2, SIDE)
 
 
-def gather_kernel(own, buf, left, send_sem, recv_sem, own_sem):
+def project_kernel(own, coulomb, out, buf, left, tile, acc, send_sem, recv_sem, own_sem):
     row, col = lax.axis_index("row"), lax.axis_index("col")
     x, y = row // SIDE, lax.rem(row, SIDE)
     z, core = col // 2, lax.rem(col, 2)
@@ -87,6 +87,8 @@
     on_z = ((row, zm * 2 + core), (row, zp * 2 + core))
     mate = (row, z * 2 + 1 - core)
     used, started = [0], []
+    tile_in = pltpu.make_async_copy(coulomb, tile, own_sem.at[2])
+    tile_in.start()
 
     def push(src, dst, device, landing):
         index = used[0]
@@ -97,10 +99,14 @@
         started.append(copy)
         return pltpu.make_async_remote_copy(landing, landing, *pair, device_id=device, device_id_type=MESH)
 
+    def left_of(at_z, at_core):
+        return left.at[at_z * 2 + at_core]
+
     greet([*on_x, *on_y, *on_z, mate])
-    local = [
-        pltpu.make_async_copy(own, buf.at[x, y], own_sem.at[0]),
-        pltpu.make_async_copy(own, left.at[z, core], own_sem.at[1]),
+    local = [pltpu.make_async_copy(own, buf.at[x, y], own_sem.at[0])]
+    local += [
+        pltpu.make_async_copy(own.at[:, q], left_of(z, core).at[:, pl.ds(64 * q, 64)], own_sem.at[1 + 2 * q])
+        for q in range(2)
     ]
     for copy in local:
         copy.start()
@@ -136,11 +142,14 @@
             push(own.at[half], here, first_to[half][0], slot(half, plus, second_at[half][1])),
         ))
     second_waits = [[(first_at[h][1], second_send(h, first_at[h][1], own.at[h]))] for h in range(2)]
+    for copy in local:
+        copy.wait()
+    mine = left_of(z, core)
     z_waits = (
-        push(own, left.at[z, core], on_z[1], left.at[zm, core]),
-        push(own, left.at[z, core], on_z[0], left.at[zp, core]),
+        push(mine, mine, on_z[1], left_of(zm, core)),
+        push(mine, mine, on_z[0], left_of(zp, core)),
     )
-    mate_waits = [push(own, left.at[z, core], mate, left.at[z, 1 - core])]
+    mate_waits = [push(mine, mine, mate, left_of(z, 1 - core))]
     first_far = []
     for half in range(2):
         for wait in first_waits[half]:
@@ -151,18 +160,50 @@
             second_waits[half].append((first_at[half][k], second_send(half, first_at[half][k])))
     for wait in z_waits:
         wait.wait_recv()
-    z_far = relay((zm, z, zp, zf), on_z, lambda at: left.at[at, core])
+    z_far = relay((zm, z, zp, zf), on_z, lambda at: left_of(at, core))
     for at in (zm, zp):
-        mate_waits.append(push(left.at[at, core], left.at[at, core], mate, left.at[at, 1 - core]))
-    last = []
-
-    def second_relay(half, first, waits):
+        mate_waits.append(push(left_of(at, core), left_of(at, core), mate, left_of(at, 1 - core)))
+    relayed = {}
+
+    def second_relay(half, k):
+        first, waits = second_waits[half][k]
         for wait in waits:
             wait.wait_recv()
-        last.extend(relay(second_at[half], second_to[half], lambda s: slot(half, first, s)))
+        relayed[half, k] = relay(second_at[half], second_to[half], lambda s: slot(half, first, s))
+
+    def landed(*keys):
+        for key in keys:
+            for wait in relayed.pop(key):
+                wait.wait_recv()
+
+    first_step = [True]
+
+    def project(one, two, final=False):
+        start = first_step[0]
+        first_step[0] = False
+
+        @pl.loop(0, left.shape[0])
+        def _(m):
+            left_rows = left[m].reshape(OWN, -1)
+            total = None
+            for bx, by in (one, two):
+                rows = buf[bx, by].reshape(OWN, -1)
+                pair = lax.dot_general(
+                    left_rows, rows, (((1,), (1,)), ((), ())), preferred_element_type=F32
+                ).astype(BF16)
+                at = pl.multiple_of((bx * SIDE + by) * OWN, OWN)
+                weights = tile[pl.ds(pl.multiple_of(m * OWN, OWN), OWN), pl.ds(at, OWN)]
+                part = jnp.dot(pair * weights, rows, preferred_element_type=F32)
+                total = part if total is None else total + part
+            if not start:
+                total = acc[m] + total
+            if final:
+                out[m] = total.astype(BF16)
+            else:
+                acc[m] = total
 
     for half in range(2):
-        second_relay(half, *second_waits[half][0])
+        second_relay(half, 0)
     for half in range(2):
         for wait in first_far[half]:
             wait.wait_recv()
@@ -170,41 +211,57 @@
         second_waits[half].append((far, second_send(half, far)))
     for wait in z_far:
         wait.wait_recv()
-    mate_waits.append(push(left.at[zf, core], left.at[zf, core], mate, left.at[zf, 1 - core]))
-    for k in (1, 2, 3):
-        for half in range(2):
-            second_relay(half, *second_waits[half][k])
-    for wait in last + mate_waits:
+    mate_waits.append(push(left_of(zf, core), left_of(zf, core), mate, left_of(zf, 1 - core)))
+    for wait in mate_waits:
         wait.wait_recv()
+    tile_in.wait()
+    project((x, y), (x, ym))
+    second_relay(0, 1)
+    second_relay(1, 1)
+    project((x, yp), (xm, y))
+    second_relay(0, 2)
+    second_relay(1, 2)
+    project((xp, y), (xm, ym))
+    second_relay(0, 3)
+    second_relay(1, 3)
+    project((xm, yp), (xp, ym))
+    landed((0, 0), (1, 0))
+    project((xp, yp), (x, yf))
+    landed((1, 1), (1, 2), (0, 1), (0, 2))
+    project((xf, y), (xm, yf))
+    project((xp, yf), (xf, ym))
+    landed((0, 3), (1, 3))
+    project((xf, yp), (xf, yf), True)
     for copy in started:
         copy.wait_send()
-    for copy in local:
-        copy.wait()
 
 
 COPIES = 2 * (4 + 4 * 4) + 4 + 4
 
 
-def gather_rows(owned_rows):
+def project_rows(owned_rows, coulomb):
     rows, norb = owned_rows.shape
     own = owned_rows.reshape(2, 2, rows // 4, norb)
+    cols = coulomb.shape[0] // rows
     vmem = pl.BlockSpec(memory_space=pltpu.VMEM)
-    buf, left = pl.pallas_call(
-        gather_kernel,
-        out_shape=(
-            jax.ShapeDtypeStruct((SIDE, SIDE, *own.shape), own.dtype),
-            jax.ShapeDtypeStruct((SIDE, 2, *own.shape), own.dtype),
-        ),
-        in_specs=[vmem],
-        out_specs=(vmem, vmem),
+    return pl.pallas_call(
+        project_kernel,
+        out_shape=jax.ShapeDtypeStruct((cols, rows, norb), BF16),
+        in_specs=[vmem, pl.BlockSpec(memory_space=pl.ANY)],
+        out_specs=vmem,
         scratch_shapes=[
+            pltpu.VMEM((SIDE, SIDE, *own.shape), BF16),
+            pltpu.VMEM((cols, 2, rows // 2, norb), BF16),
+            pltpu.VMEM(coulomb.shape, BF16),
+            pltpu.VMEM((cols, rows, norb), F32),
             pltpu.SemaphoreType.DMA((COPIES,)),
             pltpu.SemaphoreType.DMA((COPIES,)),
-            pltpu.SemaphoreType.DMA((2,)),
+            pltpu.SemaphoreType.DMA((4,)),
         ],
-        compiler_params=pltpu.CompilerParams(collective_id=1, has_side_effects=True),
-    )(own)
-    return buf.reshape(-1, norb), left.reshape(-1, norb)
+        compiler_params=pltpu.CompilerParams(
+            collective_id=1, has_side_effects=True, vmem_limit_bytes=48 * 1024 * 1024
+        ),
+    )(own, coulomb)
 
 
 STRIP = 32
@@ -261,7 +318,7 @@
 
 
 def scatter_sums(partial_sums):
-    norb = partial_sums.shape[1]
+    norb = partial_sums.shape[-1]
     vmem = pl.BlockSpec(memory_space=pltpu.VMEM)
     return pl.pallas_call(
         scatter_kernel,
@@ -283,14 +340,6 @@
 def pick(index, rows, count):
     one_hot = (index[:, None] == jnp.arange(count, dtype=jnp.int32)[None, :]).astype(BF16)
     return jnp.dot(one_hot, rows, preferred_element_type=F32).astype(BF16)
-
-
-def add_block(shard_rows, left_rows, kernel_tile):
-    pair_tile = jnp.einsum(
-        "ak,bk->ab", left_rows, shard_rows, preferred_element_type=F32
-    ).astype(BF16)
-    weighted = (pair_tile.astype(F32) * kernel_tile.astype(F32)).astype(BF16)
-    return jnp.dot(weighted, shard_rows, preferred_element_type=F32)
 
 
 def outgoing_chunks(orbitals, box_counts, owner_map, grid_rows, listed, my_box, box_total, lanes):
@@ -338,8 +387,7 @@
     owned_rows = jnp.dot(
         place, received.reshape(box_total * lanes, NORB), preferred_element_type=F32
     ).astype(BF16)
-    column_rows, left_rows = gather_rows(owned_rows)
-    partial_sums = add_block(column_rows, left_rows, coulomb).astype(BF16)
+    partial_sums = project_rows(owned_rows, coulomb)
     owned_result = scatter_sums(partial_sums)
     fetched = exchange(pick(wanted, owned_result, OWN).reshape(box_total, lanes, NORB), 3)
     return -jnp.dot(interp, fetched.reshape(LIST, NORB), preferred_element_type=F32)

time: 158 us -> 156 us (0.987)
  matrix products: 38.2 us -> 11.6 us
  Pallas kernels: 106 us -> 129 us
    pallas_call x1, Pallas kernels: 29.4 us -> 55.9 us  [project_rows(): pl.pallas_call(project_kernel, out_shape=jax.ShapeDtypeStruct((cols, rows...]
    dot_general x1 -> x0, matrix products: 25.9 us -> none  [add_block(): return jnp.dot(weighted, shard_rows, preferred_element_type=F32)]
    pallas_call x1, Pallas kernels: 19.9 us -> 15.9 us  [scatter_sums(): pl.pallas_call(scatter_kernel, out_shape=jax.ShapeDtypeStruct((OWN, norb)...]
where the time goes in v3:
time: 156 us
  Pallas kernels  129 us (83%)
  matrix products  11.6 us (7%)
  other arithmetic  7.86 us (5%)
  local copies, waits for them, and re-layouts  4.57 us (3%)
  between operations  2.19 us (1%)
    pallas_call x2, Pallas kernels, exchange(): pl.pallas_call(lambda *refs: exchange_kernel(lax.axis_size('row'), lax.ax...  57.7 us
    pallas_call x1, Pallas kernels, project_rows(): pl.pallas_call(project_kernel, out_shape=jax.ShapeDtypeStruct((cols, rows...  55.9 us
    pallas_call x1, Pallas kernels, scatter_sums(): pl.pallas_call(scatter_kernel, out_shape=jax.ShapeDtypeStruct((OWN, norb)...  15.9 us
    dot_general x2, matrix products, pick(): return jnp.dot(one_hot, rows, preferred_element_type=F32).astype(BF16)  6.09 us
    dot_general x1, matrix products, shards(): jnp.dot(interp, fetched.reshape(LIST, NORB), preferred_element_type=F32)  3.87 us

profile of v3, /device:TPU:25, one launch (start us, length us, event | category | flops | bytes accessed | tf_op | source)
XLA Modules:
  0.0 155.7 jit_solution(8503111597466655438)
XLA Ops:
  0.0 1.5 fusion.23
  3.6 0.7 iota_compare_fusion.16
  4.3 0.7 convert_reduce_fusion.3
  5.0 0.7 multiply_reduce_fusion
  5.7 0.9 subtract_add_fusion
  6.5 0.4 convert_reduce_fusion
  7.0 0.7 add_select_fusion.2
  7.6 0.4 select_reduce_fusion
  8.0 0.1 reduce_sum.42
  8.1 0.4 fusion.17
  8.5 0.1 stack_reshape_squeeze.5
  8.6 3.7 %fusion.11.refs_0_ = bf16[128,8,512]{2,1,0:T(8,128)(2,1)} fusion(bf16[1024,512]{1,0:T(8,128)(2,1)} %param.7, s32[1024]{0:T(1024)S(1)} %fusion.20, bf16[128,1,8]{2,1,0:T(2,128)(2,1)S(1)} %fusion.17, bf16[128,1,8]{2,1,0:T(2,128)(2,1)S(1)} %stack_reshape_squeeze.5, pred[8]{0:T(512)(128)(4,1)S(1)} %iota_compare_fusion.17), kind=kOutput, calls=%fused_computation.20 | convolution fusion | flops 1081606144 | bytes 2105352 | tf_op jit(solution)/shard_map/dot_general | solution.py:342
  12.3 29.2 %shard_map.73 = bf16[128,8,512]{2,1,0:T(8,128)(2,1)} custom-call(bf16[128,8,512]{2,1,0:T(8,128)(2,1)} %fusion.11.refs_0_), custom_call_target="tpu_custom_call" | custom-call | tf_op jit(solution)/shard_map/pallas_call | solution.py:66
  41.5 1.6 convert_reduce_fusion.2
  43.1 0.1 reshape.168
  43.2 0.1 reshape.169
  43.3 1.7 %convolution_convert_fusion.1 = bf16[256,512]{1,0:T(8,128)(2,1)S(1)} fusion(bf16[128,8,512]{2,1,0:T(8,128)(2,1)} %shard_map.73, s32[1024]{0:T(1024)S(1)} %reshape.169), kind=kOutput, calls=%fused_computation.21 | convolution fusion | flops 268828672 | bytes 1314816 | tf_op jit(solution)/shard_map/dot_general | solution.py:387
  44.9 55.9 %shard_map.74 = bf16[8,256,512]{2,1,0:T(8,128)(2,1)S(1)} custom-call(bf16[2,2,64,512]{3,2,1,0:T(8,128)(2,1)S(1)} %bitcast.26, bf16[2048,4096]{1,0:T(8,128)(2,1)} %coulomb.1), custom_call_target="tpu_custom_call" | custom-call | tf_op jit(solution)/shard_map/pallas_call | solution.py:247
  100.8 1.3 copy-done.1
  102.1 15.9 %shard_map.75 = bf16[256,512]{1,0:T(8,128)(2,1)} custom-call(bf16[4,2,256,512]{3,2,1,0:T(8,128)(2,1)} %bitcast.25), custom_call_target="tpu_custom_call" | custom-call | tf_op jit(solution)/shard_map/pallas_call | solution.py:323
  118.0 2.4 %fusion.9.refs_0_ = bf16[128,8,512]{2,1,0:T(8,128)(2,1)} fusion(bf16[256,512]{1,0:T(8,128)(2,1)} %shard_map.75, s32[1024]{0:T(1024)S(1)} %reshape.168), kind=kOutput, calls=%fused_computation.18 | convolution fusion | flops 269221888 | bytes 1314816 | tf_op jit(solution)/shard_map/dot_general | solution.py:342
  120.4 28.5 %shard_map.76 = bf16[128,8,512]{2,1,0:T(8,128)(2,1)} custom-call(bf16[128,8,512]{2,1,0:T(8,128)(2,1)} %fusion.9.refs_0_), custom_call_target="tpu_custom_call" | custom-call | tf_op jit(solution)/shard_map/pallas_call | solution.py:66
  148.9 3.9 %negate_bitcast_fusion = f32[1024,512]{0,1:T(8,128)} fusion(bf16[1024,1024]{1,0:T(8,128)(2,1)S(1)} %copy-done, bf16[128,8,512]{2,1,0:T(8,128)(2,1)} %shard_map.76), kind=kOutput, calls=%fused_computation.12 | convolution fusion | flops 1074266112 | bytes 5242880 | tf_op jit(solution)/shard_map/dot_general | solution.py:393
  152.8 2.9 %copy.28 = f32[1024,512]{1,0:T(8,128)} copy(f32[1024,512]{0,1:T(8,128)} %negate_bitcast_fusion) | data formatting | bytes 4194304 | tf_op jit(solution)/shard_map/neg | solution.py:393
  (5 shorter events, 0.0 us)
Async XLA Ops:
  0.0 148.9 %copy-start = (bf16[1024,1024]{1,0:T(8,128)(2,1)S(1)}, bf16[1024,1024]{1,0:T(8,128)(2,1)}, u32[]{:S(2)}) copy-start(bf16[1024,1024]{1,0:T(8,128)(2,1)} %param.9) | copy-start | bytes 6291460
  100.8 1.3 copy-start.1

commit v4 on v3

--- a/solution.py
+++ b/solution.py
@@ -18,33 +18,31 @@
 MESH = pl.DeviceIdType.MESH
 
 
-def greet(partners):
+def place(me, step):
+    count, cols = lax.axis_size("row") * lax.axis_size("col"), lax.axis_size("col")
+    other = lax.rem(me + step, count)
+    return other, (other // cols, lax.rem(other, cols))
+
+
+def greet_all(me):
+    count = lax.axis_size("row") * lax.axis_size("col")
     barrier = pltpu.get_barrier_semaphore()
-    for partner in partners:
-        pl.semaphore_signal(barrier, inc=1, device_id=partner, device_id_type=MESH)
-    pl.semaphore_wait(barrier, len(partners))
-
-
-def exchange_kernel(rows, cols, src, dst, send_sem, recv_sem, own_sem):
-    me = lax.axis_index("row") * cols + lax.axis_index("col")
-    count = rows * cols
-    barrier = pltpu.get_barrier_semaphore()
-
-    def place(step):
-        other = lax.rem(me + step, count)
-        return other, (other // cols, lax.rem(other, cols))
 
     def signal(step, carry):
-        pl.semaphore_signal(barrier, inc=1, device_id=place(step)[1], device_id_type=MESH)
+        pl.semaphore_signal(barrier, inc=1, device_id=place(me, step)[1], device_id_type=MESH)
         return carry
 
     lax.fori_loop(1, count, signal, 0)
+    pl.semaphore_wait(barrier, count - 1)
+
+
+def send_all(me, src, dst, send_sem, recv_sem, own_sem):
+    count = lax.axis_size("row") * lax.axis_size("col")
     own = pltpu.make_async_copy(src.at[me], dst.at[me], own_sem)
     own.start()
-    pl.semaphore_wait(barrier, count - 1)
 
     def send(step, carry):
-        other, device = place(step)
+        other, device = place(me, step)
         pltpu.make_async_remote_copy(
             src_ref=src.at[other],
             dst_ref=dst.at[me],
@@ -62,9 +60,15 @@
     pltpu.make_async_copy(src.at[many], dst.at[many], recv_sem).wait()
 
 
+def exchange_kernel(src, dst, *sems):
+    me = lax.axis_index("row") * lax.axis_size("col") + lax.axis_index("col")
+    greet_all(me)
+    send_all(me, src, dst, *sems)
+
+
 def exchange(chunks, collective_id):
     return pl.pallas_call(
-        lambda *refs: exchange_kernel(lax.axis_size("row"), lax.axis_size("col"), *refs),
+        exchange_kernel,
         out_shape=jax.ShapeDtypeStruct(chunks.shape, chunks.dtype),
         in_specs=[pl.BlockSpec(memory_space=pltpu.VMEM)],
         out_specs=pl.BlockSpec(memory_space=pltpu.VMEM),
@@ -77,7 +81,10 @@
     return lax.rem(at + SIDE - 1, SIDE), lax.rem(at + 1, SIDE), lax.rem(at + 2, SIDE)
 
 
-def project_kernel(own, coulomb, out, buf, left, tile, acc, send_sem, recv_sem, own_sem):
+def project_kernel(
+    own, coulomb, chosen, out, buf, left, tile, acc, part, inbox, stage, halves, blocks, result, outgoing,
+    send_sem, recv_sem, own_sem, sum_send, sum_recv, *out_sems
+):
     row, col = lax.axis_index("row"), lax.axis_index("col")
     x, y = row // SIDE, lax.rem(row, SIDE)
     z, core = col // 2, lax.rem(col, 2)
@@ -102,7 +109,8 @@
     def left_of(at_z, at_core):
         return left.at[at_z * 2 + at_core]
 
-    greet([*on_x, *on_y, *on_z, mate])
+    me = row * lax.axis_size("col") + col
+    greet_all(me)
     local = [pltpu.make_async_copy(own, buf.at[x, y], own_sem.at[0])]
     local += [
         pltpu.make_async_copy(own.at[:, q], left_of(z, core).at[:, pl.ds(64 * q, 64)], own_sem.at[1 + 2 * q])
@@ -178,29 +186,30 @@
 
     first_step = [True]
 
-    def project(one, two, final=False):
+    def project_at(at_z, one, two, start, final):
+        left_rows = left[pl.ds(at_z * 2, 2)].reshape(2 * OWN, -1)
+        total = None if start else acc[at_z]
+        for bx, by in (one, two):
+            rows = buf[bx, by].reshape(OWN, -1)
+            pair = lax.dot_general(
+                left_rows, rows, (((1,), (1,)), ((), ())), preferred_element_type=F32
+            ).astype(BF16)
+            at = pl.multiple_of((bx * SIDE + by) * OWN, OWN)
+            weights = tile[pl.ds(pl.multiple_of(at_z * 2 * OWN, 2 * OWN), 2 * OWN), pl.ds(at, OWN)]
+            term = jnp.dot(pair * weights, rows, preferred_element_type=F32)
+            total = term if total is None else total + term
+        if final:
+            part[at_z] = total.astype(BF16).reshape(2, OWN, -1)
+        else:
+            acc[at_z] = total
+
+    def project(one, two):
         start = first_step[0]
         first_step[0] = False
 
-        @pl.loop(0, left.shape[0])
-        def _(m):
-            left_rows = left[m].reshape(OWN, -1)
-            total = None
-            for bx, by in (one, two):
-                rows = buf[bx, by].reshape(OWN, -1)
-                pair = lax.dot_general(
-                    left_rows, rows, (((1,), (1,)), ((), ())), preferred_element_type=F32
-                ).astype(BF16)
-                at = pl.multiple_of((bx * SIDE + by) * OWN, OWN)
-                weights = tile[pl.ds(pl.multiple_of(m * OWN, OWN), OWN), pl.ds(at, OWN)]
-                part = jnp.dot(pair * weights, rows, preferred_element_type=F32)
-                total = part if total is None else total + part
-            if not start:
-                total = acc[m] + total
-            if final:
-                out[m] = total.astype(BF16)
-            else:
-                acc[m] = total
+        @pl.loop(0, SIDE)
+        def _(at_z):
+            project_at(at_z, one, two, start, False)
 
     for half in range(2):
         second_relay(half, 0)
@@ -231,110 +240,96 @@
     project((xf, y), (xm, yf))
     project((xp, yf), (xf, ym))
     landed((0, 3), (1, 3))
-    project((xf, yp), (xf, yf), True)
-    for copy in started:
-        copy.wait_send()
-
-
-COPIES = 2 * (4 + 4 * 4) + 4 + 4
-
-
-def project_rows(owned_rows, coulomb):
-    rows, norb = owned_rows.shape
-    own = owned_rows.reshape(2, 2, rows // 4, norb)
-    cols = coulomb.shape[0] // rows
-    vmem = pl.BlockSpec(memory_space=pltpu.VMEM)
-    return pl.pallas_call(
-        project_kernel,
-        out_shape=jax.ShapeDtypeStruct((cols, rows, norb), BF16),
-        in_specs=[vmem, pl.BlockSpec(memory_space=pl.ANY)],
-        out_specs=vmem,
-        scratch_shapes=[
-            pltpu.VMEM((SIDE, SIDE, *own.shape), BF16),
-            pltpu.VMEM((cols, 2, rows // 2, norb), BF16),
-            pltpu.VMEM(coulomb.shape, BF16),
-            pltpu.VMEM((cols, rows, norb), F32),
-            pltpu.SemaphoreType.DMA((COPIES,)),
-            pltpu.SemaphoreType.DMA((COPIES,)),
-            pltpu.SemaphoreType.DMA((4,)),
-        ],
-        compiler_params=pltpu.CompilerParams(
-            collective_id=1, has_side_effects=True, vmem_limit_bytes=48 * 1024 * 1024
-        ),
-    )(own, coulomb)
-
-
-STRIP = 32
-
-
-def scatter_kernel(src, out, inbox, stage, halves, blocks, send_sem, recv_sem):
-    row, col = lax.axis_index("row"), lax.axis_index("col")
-    z, core = col // 2, lax.rem(col, 2)
-    zm, zp, zf = around(z)
-    minus, plus = (row, zm * 2 + core), (row, zp * 2 + core)
-    mate = (row, z * 2 + 1 - core)
-    half = src.shape[2] // 2
-    greet([minus, plus, mate])
-
-    def push(index, src_ref, dst_ref, device):
+    def sum_push(index, src_ref, dst_ref, device):
         copy = pltpu.make_async_remote_copy(
-            src_ref, dst_ref, send_sem.at[index], recv_sem.at[index], device_id=device, device_id_type=MESH
+            src_ref, dst_ref, sum_send.at[index], sum_recv.at[index], device_id=device, device_id_type=MESH
         )
         copy.start()
         return copy
 
-    mates = [push(i, src.at[at, 1 - core], inbox.at[at], mate) for i, at in enumerate((zf, zp, zm, z))]
+    mates = []
+    for index, at in enumerate((zf, zp, zm, z)):
+        project_at(at, (xf, yp), (xf, yf), False, True)
+        mates.append(sum_push(index, part.at[at, 1 - core], inbox.at[at], mate))
+    half = OWN // 2
+    plus, minus = on_z[1], on_z[0]
 
     def add(at, start, size, write, *more):
         @pl.loop(0, size // STRIP)
         def _(i):
             rows = pl.ds(pl.multiple_of(start + i * STRIP, STRIP), STRIP)
-            total = src[at, core, rows, :].astype(F32) + inbox[at, rows, :].astype(F32)
+            total = part[at, core, rows, :].astype(F32) + inbox[at, rows, :].astype(F32)
             for ref, shift in more:
-                part = pl.ds(pl.multiple_of(start - shift + i * STRIP, STRIP), STRIP)
-                total += ref[part, :].astype(F32)
+                piece = pl.ds(pl.multiple_of(start - shift + i * STRIP, STRIP), STRIP)
+                total += ref[piece, :].astype(F32)
             write[rows, :] = total.astype(BF16)
 
     mates[0].wait_recv()
     add(zf, 0, 2 * half, stage.at[0])
-    up = push(4, stage.at[0, pl.ds(0, half)], halves.at[0], plus)
-    down = push(5, stage.at[0, pl.ds(half, half)], halves.at[1], minus)
+    up = sum_push(4, stage.at[0, pl.ds(0, half)], halves.at[0], plus)
+    down = sum_push(5, stage.at[0, pl.ds(half, half)], halves.at[1], minus)
     mates[1].wait_recv()
     add(zp, half, half, stage.at[1])
     mates[2].wait_recv()
     add(zm, 0, half, stage.at[2])
     up.wait_recv()
     add(zp, 0, half, stage.at[1], (halves.at[0], 0))
-    up_block = push(6, stage.at[1], blocks.at[0], plus)
+    up_block = sum_push(6, stage.at[1], blocks.at[0], plus)
     down.wait_recv()
     add(zm, half, half, stage.at[2], (halves.at[1], half))
-    down_block = push(7, stage.at[2], blocks.at[1], minus)
+    down_block = sum_push(7, stage.at[2], blocks.at[1], minus)
     mates[3].wait_recv()
     up_block.wait_recv()
     down_block.wait_recv()
-    add(z, 0, 2 * half, out, (blocks.at[0], 0), (blocks.at[1], 0))
+    add(z, 0, 2 * half, result, (blocks.at[0], 0), (blocks.at[1], 0))
     for copy in (*mates, up, down, up_block, down_block):
         copy.wait_send()
-
-
-def scatter_sums(partial_sums):
-    norb = partial_sums.shape[-1]
+    for i in range(outgoing.shape[0] * outgoing.shape[1] // OWN):
+        boxes = OWN // outgoing.shape[1]
+        picked = jnp.dot(chosen[pl.ds(i * OWN, OWN), :], result[...], preferred_element_type=F32)
+        outgoing[pl.ds(i * boxes, boxes)] = picked.reshape(boxes, outgoing.shape[1], -1).astype(BF16)
+    send_all(me, outgoing, out, *out_sems)
+    for copy in started:
+        copy.wait_send()
+
+
+STRIP = 32
+COPIES = 2 * (4 + 4 * 4) + 4 + 4
+
+
+def project_rows(owned_rows, coulomb, chosen, boxes):
+    rows, norb = owned_rows.shape
+    own = owned_rows.reshape(2, 2, rows // 4, norb)
+    out = (boxes, chosen.shape[0] // boxes, norb)
     vmem = pl.BlockSpec(memory_space=pltpu.VMEM)
     return pl.pallas_call(
-        scatter_kernel,
-        out_shape=jax.ShapeDtypeStruct((OWN, norb), BF16),
-        in_specs=[vmem],
+        project_kernel,
+        out_shape=jax.ShapeDtypeStruct(out, BF16),
+        in_specs=[vmem, pl.BlockSpec(memory_space=pl.ANY), vmem],
         out_specs=vmem,
         scratch_shapes=[
-            pltpu.VMEM((SIDE, OWN, norb), BF16),
-            pltpu.VMEM((3, OWN, norb), BF16),
-            pltpu.VMEM((2, OWN // 2, norb), BF16),
-            pltpu.VMEM((2, OWN, norb), BF16),
+            pltpu.VMEM((SIDE, SIDE, *own.shape), BF16),
+            pltpu.VMEM((SIDE * 2, 2, rows // 2, norb), BF16),
+            pltpu.VMEM(coulomb.shape, BF16),
+            pltpu.VMEM((SIDE, 2 * rows, norb), F32),
+            pltpu.VMEM((SIDE, 2, rows, norb), BF16),
+            pltpu.VMEM((SIDE, rows, norb), BF16),
+            pltpu.VMEM((3, rows, norb), BF16),
+            pltpu.VMEM((2, rows // 2, norb), BF16),
+            pltpu.VMEM((2, rows, norb), BF16),
+            pltpu.VMEM((rows, norb), BF16),
+            pltpu.VMEM(out, BF16),
+            pltpu.SemaphoreType.DMA((COPIES,)),
+            pltpu.SemaphoreType.DMA((COPIES,)),
+            pltpu.SemaphoreType.DMA((4,)),
             pltpu.SemaphoreType.DMA((8,)),
             pltpu.SemaphoreType.DMA((8,)),
+            *[pltpu.SemaphoreType.DMA] * 3,
         ],
-        compiler_params=pltpu.CompilerParams(collective_id=2, has_side_effects=True),
-    )(partial_sums.reshape(SIDE, 2, OWN, norb))
+        compiler_params=pltpu.CompilerParams(
+            collective_id=1, has_side_effects=True, vmem_limit_bytes=56 * 1024 * 1024
+        ),
+    )(own, coulomb, chosen)
 
 
 def pick(index, rows, count):
@@ -387,9 +382,8 @@
     owned_rows = jnp.dot(
         place, received.reshape(box_total * lanes, NORB), preferred_element_type=F32
     ).astype(BF16)
-    partial_sums = project_rows(owned_rows, coulomb)
-    owned_result = scatter_sums(partial_sums)
-    fetched = exchange(pick(wanted, owned_result, OWN).reshape(box_total, lanes, NORB), 3)
+    chosen = (wanted[:, None] == jnp.arange(OWN, dtype=jnp.int32)[None, :]).astype(BF16)
+    fetched = project_rows(owned_rows, coulomb, chosen, box_total)
     return -jnp.dot(interp, fetched.reshape(LIST, NORB), preferred_element_type=F32)
 
 

time: 156 us -> 145 us (0.929)
  Pallas kernels: 129 us -> 120 us
  matrix products: 11.6 us -> 9.94 us
    pallas_call x4 -> x2, Pallas kernels: 129 us -> 120 us  [the longest x1 90.5 us: project_rows(): pl.pallas_call(project_kernel, out_shape=jax.ShapeDtypeStruct(out, BF16),...]
    dot_general x2 -> x1, matrix products: 6.09 us -> 3.68 us  [pick(): return jnp.dot(one_hot, rows, preferred_element_type=F32).astype(BF16)]
where the time goes in v4:
time: 145 us; the launch traced here: 144 us
  Pallas kernels  120 us (83%)
  matrix products  9.94 us (7%)
  other arithmetic  8.85 us (6%)
  local copies, waits for them, and re-layouts  3.26 us (2%)
  between operations  2.16 us (1%)
    pallas_call x1, Pallas kernels, project_rows(): pl.pallas_call(project_kernel, out_shape=jax.ShapeDtypeStruct(out, BF16),...  90.5 us
    pallas_call x1, Pallas kernels, exchange(): pl.pallas_call(exchange_kernel, out_shape=jax.ShapeDtypeStruct(chunks.sha...  29.3 us
    dot_general x1, matrix products, shards(): jnp.dot(interp, fetched.reshape(LIST, NORB), preferred_element_type=F32)  3.87 us
    dot_general x1, matrix products, pick(): return jnp.dot(one_hot, rows, preferred_element_type=F32).astype(BF16)  3.68 us

profile of v4, /device:TPU:25, one launch (start us, length us, event | category | flops | bytes accessed | tf_op | source)
XLA Modules:
  0.0 144.0 jit_solution(17431958224491477057)
XLA Ops:
  0.0 0.0 copy-start
  0.0 1.5 %fusion.22 = (s32[]{:T(128)}, s32[]{:T(128)}) fusion(s32[128]{0:T(128)} %param.10, s32[]{:T(128)S(6)} %add.46), kind=kLoop, calls=%fused_computation.58 | loop fusion | flops 766 | bytes 524 | tf_op jit(solution)/shard_map/reduce_sum | solution.py:344
  3.6 0.7 iota_compare_fusion.15
  4.3 0.7 convert_reduce_fusion.3
  5.0 0.7 multiply_reduce_fusion
  5.7 0.9 subtract_add_fusion
  6.5 0.4 convert_reduce_fusion
  7.0 0.7 add_select_fusion.2
  7.6 0.4 select_reduce_fusion
  8.0 0.1 reduce_sum.42
  8.1 0.4 fusion.16
  8.5 0.1 stack_reshape_squeeze.5
  8.6 3.7 %fusion.10.src = bf16[128,8,512]{2,1,0:T(8,128)(2,1)} fusion(bf16[1024,512]{1,0:T(8,128)(2,1)} %param.7, s32[1024]{0:T(1024)S(1)} %fusion.19, bf16[128,1,8]{2,1,0:T(2,128)(2,1)S(1)} %fusion.16, bf16[128,1,8]{2,1,0:T(2,128)(2,1)S(1)} %stack_reshape_squeeze.5, pred[8]{0:T(512)(128)(4,1)S(1)} %iota_compare_fusion.16), kind=kOutput, calls=%fused_computation.18 | convolution fusion | flops 1081606144 | bytes 2105352 | tf_op jit(solution)/shard_map/dot_general | solution.py:337
  12.3 29.3 %shard_map.73 = bf16[128,8,512]{2,1,0:T(8,128)(2,1)} custom-call(bf16[128,8,512]{2,1,0:T(8,128)(2,1)} %fusion.10.src), custom_call_target="tpu_custom_call" | custom-call | tf_op jit(solution)/shard_map/pallas_call | solution.py:70
  41.6 1.6 %convert_reduce_fusion.1 = (s32[128,8]{1,0:T(8,128)S(1)}, s32[128,8]{1,0:T(8,128)S(1)}) fusion(bf16[128,8,512]{2,1,0:T(8,128)(2,1)} %shard_map.73), kind=kLoop, calls=%fused_computation.34 | loop fusion | flops 2048 | bytes 12288 | tf_op jit(solution)/shard_map/convert_element_type | solution.py:379
  43.2 0.1 reshape.161
  43.3 0.1 reshape.160
  43.4 2.4 %convolution_convert_fusion = bf16[256,512]{1,0:T(8,128)(2,1)} fusion(bf16[128,8,512]{2,1,0:T(8,128)(2,1)} %shard_map.73, s32[1024]{0:T(1024)S(1)} %reshape.160), kind=kOutput, calls=%fused_computation.19 | convolution fusion | flops 268828672 | bytes 1314816 | tf_op jit(solution)/shard_map/dot_general | solution.py:382
  45.7 1.0 fusion.14.chosen
  46.7 90.5 %shard_map.74 = bf16[128,8,512]{2,1,0:T(8,128)(2,1)} custom-call(bf16[2,2,64,512]{3,2,1,0:T(8,128)(2,1)} %bitcast.21, bf16[2048,4096]{1,0:T(8,128)(2,1)} %coulomb.1, bf16[1024,256]{1,0:T(8,128)(2,1)} %fusion.14.chosen), custom_call_target="tpu_custom_call" | custom-call | tf_op jit(solution)/shard_map/pallas_call | solution.py:305
  137.3 0.0 copy-done
  137.3 3.9 %negate_bitcast_fusion = f32[1024,512]{0,1:T(8,128)} fusion(bf16[1024,1024]{1,0:T(8,128)(2,1)S(1)} %copy-done, bf16[128,8,512]{2,1,0:T(8,128)(2,1)} %shard_map.74), kind=kOutput, calls=%fused_computation.12 | convolution fusion | flops 1074266112 | bytes 5242880 | tf_op jit(solution)/shard_map/dot_general | solution.py:387
  141.1 2.9 %copy.28 = f32[1024,512]{1,0:T(8,128)} copy(f32[1024,512]{0,1:T(8,128)} %negate_bitcast_fusion) | data formatting | bytes 4194304 | tf_op jit(solution)/shard_map/neg | solution.py:387
  (2 shorter events, 0.0 us)
Async XLA Ops:
  0.0 137.3 %copy-start = (bf16[1024,1024]{1,0:T(8,128)(2,1)S(1)}, bf16[1024,1024]{1,0:T(8,128)(2,1)}, u32[]{:S(2)}) copy-start(bf16[1024,1024]{1,0:T(8,128)(2,1)} %param.9) | copy-start | bytes 6291460

commit v5 on v4

--- a/solution.py
+++ b/solution.py
@@ -15,12 +15,13 @@
 
 
 SIDE = 4
+STRIDE = 37
 MESH = pl.DeviceIdType.MESH
 
 
 def place(me, step):
     count, cols = lax.axis_size("row") * lax.axis_size("col"), lax.axis_size("col")
-    other = lax.rem(me + step, count)
+    other = lax.rem(me + STRIDE * step, count)
     return other, (other // cols, lax.rem(other, cols))
 
 
@@ -225,14 +226,13 @@
         wait.wait_recv()
     tile_in.wait()
     project((x, y), (x, ym))
-    second_relay(0, 1)
-    second_relay(1, 1)
+    for k in (1, 2):
+        second_relay(0, k)
+        second_relay(1, k)
     project((x, yp), (xm, y))
-    second_relay(0, 2)
-    second_relay(1, 2)
-    project((xp, y), (xm, ym))
     second_relay(0, 3)
     second_relay(1, 3)
+    project((xp, y), (xm, ym))
     project((xm, yp), (xp, ym))
     landed((0, 0), (1, 0))
     project((xp, yp), (x, yf))
@@ -332,6 +332,23 @@
     )(own, coulomb, chosen)
 
 
+def action_kernel(interp, rows, out):
+    out[...] = -jnp.dot(interp[...], rows[...], preferred_element_type=F32)
+
+
+def action(interp, rows):
+    count, listed = interp.shape
+    norb = rows.shape[1]
+    block = count // 4
+    return pl.pallas_call(
+        action_kernel,
+        grid=(4,),
+        out_shape=jax.ShapeDtypeStruct((count, norb), F32),
+        in_specs=[pl.BlockSpec((block, listed), lambda i: (i, 0)), pl.BlockSpec((listed, norb), lambda i: (0, 0))],
+        out_specs=pl.BlockSpec((block, norb), lambda i: (i, 0)),
+    )(interp, rows)
+
+
 def pick(index, rows, count):
     one_hot = (index[:, None] == jnp.arange(count, dtype=jnp.int32)[None, :]).astype(BF16)
     return jnp.dot(one_hot, rows, preferred_element_type=F32).astype(BF16)
@@ -384,7 +401,7 @@
     ).astype(BF16)
     chosen = (wanted[:, None] == jnp.arange(OWN, dtype=jnp.int32)[None, :]).astype(BF16)
     fetched = project_rows(owned_rows, coulomb, chosen, box_total)
-    return -jnp.dot(interp, fetched.reshape(LIST, NORB), preferred_element_type=F32)
+    return action(interp, fetched.reshape(LIST, NORB))
 
 
 def solution(mesh):

time: 145 us -> 138 us (0.952)
  matrix products: 9.94 us -> 4.86 us
  local copies, waits for them, and re-layouts: 3.26 us -> 0.38 us
    pallas_call x0 -> x1, Pallas kernels: none -> 4.95 us  [action(): pl.pallas_call(action_kernel, grid=(4,), out_shape=jax.ShapeDtypeStruct((...]
    dot_general x1 -> x0, matrix products: 3.87 us -> none  [shards(): jnp.dot(interp, fetched.reshape(LIST, NORB), preferred_element_type=F32)]
    pallas_call x1, Pallas kernels: 29.3 us -> 26.3 us  [exchange(): pl.pallas_call(exchange_kernel, out_shape=jax.ShapeDtypeStruct(chunks.sha...]
    neg x1 -> x0, local copies, waits for them, and re-layouts: 2.88 us -> none  [shards(): -jnp.dot(interp, fetched.reshape(LIST, NORB), preferred_element_type=F32)]
    pallas_call x1, Pallas kernels: 90.5 us -> 88.5 us  [project_rows(): pl.pallas_call(project_kernel, out_shape=jax.ShapeDtypeStruct(out, BF16),...]
where the time goes in v5:
time: 138 us; the launch traced here: 136 us
  Pallas kernels  120 us (87%)
  other arithmetic  8.79 us (6%)
  matrix products  4.86 us (4%)
  between operations  2.16 us (2%)
    pallas_call x1, Pallas kernels, project_rows(): pl.pallas_call(project_kernel, out_shape=jax.ShapeDtypeStruct(out, BF16),...  88.5 us
    pallas_call x1, Pallas kernels, exchange(): pl.pallas_call(exchange_kernel, out_shape=jax.ShapeDtypeStruct(chunks.sha...  26.3 us
    pallas_call x1, Pallas kernels, action(): pl.pallas_call(action_kernel, grid=(4,), out_shape=jax.ShapeDtypeStruct((...  4.95 us

profile of v5, /device:TPU:25, one launch (start us, length us, event | category | flops | bytes accessed | tf_op | source)
XLA Modules:
  0.0 135.9 jit_solution(3618983989524545729)
XLA Ops:
  0.0 0.0 copy-start
  0.0 1.5 %fusion.21 = (s32[]{:T(128)}, s32[]{:T(128)}) fusion(s32[128]{0:T(128)} %param.10, s32[]{:T(128)S(6)} %add.46), kind=kLoop, calls=%fused_computation.56 | loop fusion | flops 766 | bytes 524 | tf_op jit(solution)/shard_map/reduce_sum | solution.py:361
  3.6 0.7 iota_compare_fusion.15
  4.2 0.7 convert_reduce_fusion.3
  4.9 0.7 multiply_reduce_fusion
  5.6 0.9 subtract_add_fusion
  6.5 0.4 convert_reduce_fusion
  6.9 0.7 add_select_fusion.2
  7.6 0.4 select_reduce_fusion
  8.0 0.1 reduce_sum.42
  8.1 0.4 fusion.15
  8.4 0.1 stack_reshape_squeeze.5
  8.6 0.0 copy-done
  8.6 2.5 %fusion.10.src = bf16[128,8,512]{2,1,0:T(8,128)(2,1)} fusion(bf16[1024,512]{1,0:T(8,128)(2,1)S(1)} %copy-done, s32[1024]{0:T(1024)S(1)} %fusion.18, bf16[128,1,8]{2,1,0:T(2,128)(2,1)S(1)} %fusion.15, bf16[128,1,8]{2,1,0:T(2,128)(2,1)S(1)} %stack_reshape_squeeze.5, pred[8]{0:T(512)(128)(4,1)S(1)} %iota_compare_fusion.16), kind=kOutput, calls=%fused_computation.17 | convolution fusion | flops 1081606144 | bytes 2105352 | tf_op jit(solution)/shard_map/dot_general | solution.py:354
  11.0 26.3 %shard_map.73 = bf16[128,8,512]{2,1,0:T(8,128)(2,1)} custom-call(bf16[128,8,512]{2,1,0:T(8,128)(2,1)} %fusion.10.src), custom_call_target="tpu_custom_call" | custom-call | tf_op jit(solution)/shard_map/pallas_call | solution.py:71
  37.3 1.6 %convert_reduce_fusion.1 = (s32[128,8]{1,0:T(8,128)S(1)}, s32[128,8]{1,0:T(8,128)S(1)}) fusion(bf16[128,8,512]{2,1,0:T(8,128)(2,1)} %shard_map.73), kind=kLoop, calls=%fused_computation.32 | loop fusion | flops 2048 | bytes 12288 | tf_op jit(solution)/shard_map/convert_element_type | solution.py:396
  38.9 0.1 reshape.161
  39.0 0.1 reshape.160
  39.1 2.4 %convolution_convert_fusion = bf16[256,512]{1,0:T(8,128)(2,1)} fusion(bf16[128,8,512]{2,1,0:T(8,128)(2,1)} %shard_map.73, s32[1024]{0:T(1024)S(1)} %reshape.160), kind=kOutput, calls=%fused_computation.18 | convolution fusion | flops 268828672 | bytes 1314816 | tf_op jit(solution)/shard_map/dot_general | solution.py:399
  41.5 1.0 fusion.13.chosen
  42.5 88.5 %shard_map.74 = bf16[128,8,512]{2,1,0:T(8,128)(2,1)} custom-call(bf16[2,2,64,512]{3,2,1,0:T(8,128)(2,1)} %bitcast.17, bf16[2048,4096]{1,0:T(8,128)(2,1)} %coulomb.1, bf16[1024,256]{1,0:T(8,128)(2,1)} %fusion.13.chosen), custom_call_target="tpu_custom_call" | custom-call | tf_op jit(solution)/shard_map/pallas_call | solution.py:305
  130.9 4.9 %shard_map.75 = f32[1024,512]{1,0:T(8,128)} custom-call(bf16[1024,1024]{1,0:T(8,128)(2,1)} %interp.1, bf16[1024,512]{1,0:T(8,128)(2,1)} %bitcast.16), custom_call_target="tpu_custom_call" | custom-call | tf_op jit(solution)/shard_map/pallas_call | solution.py:343
  (2 shorter events, 0.0 us)
Async XLA Ops:
  0.0 8.6 %copy-start = (bf16[1024,512]{1,0:T(8,128)(2,1)S(1)}, bf16[1024,512]{1,0:T(8,128)(2,1)}, u32[]{:S(2)}) copy-start(bf16[1024,512]{1,0:T(8,128)(2,1)} %param.7) | copy-start | bytes 3145732

commit v6 on v5

--- a/solution.py
+++ b/solution.py
@@ -25,7 +25,7 @@
     return other, (other // cols, lax.rem(other, cols))
 
 
-def greet_all(me):
+def greet_all(me, meanwhile=None):
     count = lax.axis_size("row") * lax.axis_size("col")
     barrier = pltpu.get_barrier_semaphore()
 
@@ -34,6 +34,8 @@
         return carry
 
     lax.fori_loop(1, count, signal, 0)
+    if meanwhile is not None:
+        meanwhile()
     pl.semaphore_wait(barrier, count - 1)
 
 
@@ -61,21 +63,31 @@
     pltpu.make_async_copy(src.at[many], dst.at[many], recv_sem).wait()
 
 
-def exchange_kernel(src, dst, *sems):
+def exchange_kernel(index, rows, meta, dst, src, *sems):
     me = lax.axis_index("row") * lax.axis_size("col") + lax.axis_index("col")
-    greet_all(me)
+    boxes = OWN // src.shape[1]
+
+    def fill():
+        for i in range(index.shape[0] // OWN):
+            places = lax.broadcasted_iota(jnp.int32, (OWN, rows.shape[0]), 1)
+            one_hot = (index[pl.ds(i * OWN, OWN), :] == places).astype(F32).astype(BF16)
+            picked = jnp.dot(one_hot, rows[...], preferred_element_type=F32)
+            at = pl.ds(i * boxes, boxes)
+            src[at] = (picked.reshape(boxes, src.shape[1], -1) + meta[at].astype(F32)).astype(BF16)
+
+    greet_all(me, fill)
     send_all(me, src, dst, *sems)
 
 
-def exchange(chunks, collective_id):
+def exchange(index, rows, meta):
     return pl.pallas_call(
         exchange_kernel,
-        out_shape=jax.ShapeDtypeStruct(chunks.shape, chunks.dtype),
-        in_specs=[pl.BlockSpec(memory_space=pltpu.VMEM)],
+        out_shape=jax.ShapeDtypeStruct(meta.shape, meta.dtype),
+        in_specs=[pl.BlockSpec(memory_space=pltpu.VMEM)] * 3,
         out_specs=pl.BlockSpec(memory_space=pltpu.VMEM),
-        scratch_shapes=[pltpu.SemaphoreType.DMA] * 3,
-        compiler_params=pltpu.CompilerParams(collective_id=collective_id, has_side_effects=True),
-    )(chunks)
+        scratch_shapes=[pltpu.VMEM(meta.shape, meta.dtype)] + [pltpu.SemaphoreType.DMA] * 3,
+        compiler_params=pltpu.CompilerParams(collective_id=0, has_side_effects=True),
+    )(index[:, None], rows, meta)
 
 
 def around(at):
@@ -378,11 +390,9 @@
     found = jnp.sum(jnp.where(hits, coded[None, :], 0), axis=1)
     grid = found // OWN - 1
     local = jnp.where(found > 0, found - (grid + 1) * OWN, -1)
-    picked = pick(grid, orbitals, orbitals.shape[0]).reshape(box_total, lanes, NORB)
     meta = jnp.stack([listed[0].reshape(box_total, per_owner), local.reshape(box_total, lanes)], axis=1)
     meta = jnp.pad(meta.astype(BF16), ((0, 0), (lanes - 2, 0), (0, NORB - per_owner)))
-    row_ids = jnp.arange(lanes)[None, :, None]
-    return jnp.where(row_ids < lanes - 2, picked, meta)
+    return grid, orbitals, meta
 
 
 def shards(orbitals, coulomb, interp, box_counts, owner_map, grid_rows, listed):
@@ -390,8 +400,7 @@
     lanes = LIST // box_total
     my_box = lax.axis_index("row") * lax.axis_size("col") + lax.axis_index("col")
     received = exchange(
-        outgoing_chunks(orbitals, box_counts, owner_map, grid_rows, listed, my_box, box_total, lanes),
-        0,
+        *outgoing_chunks(orbitals, box_counts, owner_map, grid_rows, listed, my_box, box_total, lanes)
     )
     wanted = received[:, lanes - 2, :lanes].astype(jnp.int32).reshape(-1)
     local = received[:, lanes - 1, :lanes].astype(jnp.int32).reshape(-1)

time: 138 us -> 139 us (level)
  matrix products: 4.86 us -> 2.38 us
  other arithmetic: 8.79 us -> 11.1 us
    dot_general x1 -> x0, matrix products: 2.46 us -> none  [pick(): return jnp.dot(one_hot, rows, preferred_element_type=F32).astype(BF16)]
where the time goes in v6:
time: 139 us; the launch traced here: 136 us
  Pallas kernels  120 us (86%)
  other arithmetic  11.1 us (8%)
  matrix products  2.38 us (2%)
  between operations  2.15 us (2%)
    pallas_call x1, Pallas kernels, project_rows(): pl.pallas_call(project_kernel, out_shape=jax.ShapeDtypeStruct(out, BF16),...  88.5 us
    pallas_call x1, Pallas kernels, exchange(): pl.pallas_call(exchange_kernel, out_shape=jax.ShapeDtypeStruct(meta.shape...  26.8 us
    pallas_call x1, Pallas kernels, action(): pl.pallas_call(action_kernel, grid=(4,), out_shape=jax.ShapeDtypeStruct((...  4.95 us

profile of v6, /device:TPU:25, one launch (start us, length us, event | category | flops | bytes accessed | tf_op | source)
XLA Modules:
  0.0 136.5 jit_solution(13157281291043082029)
XLA Ops:
  0.0 1.4 %fusion.16 = (s32[]{:T(128)}, s32[]{:T(128)}) fusion(s32[128]{0:T(128)} %param.10, s32[]{:T(128)S(6)} %add.52), kind=kLoop, calls=%fused_computation.50 | loop fusion | flops 766 | bytes 524 | tf_op jit(solution)/shard_map/reduce_sum | solution.py:373
  3.5 0.7 iota_compare_fusion.7
  4.1 0.7 convert_reduce_fusion.3
  4.8 0.7 multiply_reduce_fusion
  5.5 0.9 subtract_add_fusion
  6.4 0.4 convert_reduce_fusion
  6.8 0.7 add_select_fusion.2
  7.5 0.4 select_reduce_fusion
  7.9 0.1 stack_reshape_squeeze.5
  8.0 0.1 reduce_sum.45
  8.1 0.4 fusion.13
  8.5 0.2 copy.26
  8.7 1.1 fusion.10.index
  9.8 1.3 fusion.6.meta
  11.1 26.8 %shard_map.73 = bf16[128,8,512]{2,1,0:T(8,128)(2,1)} custom-call(s32[1024,1]{1,0:T(8,128)} %fusion.10.index, bf16[1024,512]{1,0:T(8,128)(2,1)} %rows.1, bf16[128,8,512]{2,1,0:T(8,128)(2,1)} %fusion.6.meta), custom_call_target="tpu_custom_call" | custom-call | tf_op jit(solution)/shard_map/pallas_call | solution.py:83
  37.9 1.6 %convert_reduce_fusion.1 = (s32[128,8]{1,0:T(8,128)S(1)}, s32[128,8]{1,0:T(8,128)S(1)}) fusion(bf16[128,8,512]{2,1,0:T(8,128)(2,1)} %shard_map.73), kind=kLoop, calls=%fused_computation.34 | loop fusion | flops 2048 | bytes 12288 | tf_op jit(solution)/shard_map/convert_element_type | solution.py:405
  39.5 0.1 reshape.186
  39.5 0.1 reshape.185
  39.6 2.4 %convolution_convert_fusion = bf16[256,512]{1,0:T(8,128)(2,1)} fusion(bf16[128,8,512]{2,1,0:T(8,128)(2,1)} %shard_map.73, s32[1024]{0:T(1024)S(1)} %reshape.185), kind=kOutput, calls=%fused_computation.12 | convolution fusion | flops 268828672 | bytes 1314816 | tf_op jit(solution)/shard_map/dot_general | solution.py:408
  42.0 1.0 fusion.8.chosen
  43.0 88.5 %shard_map.74 = bf16[128,8,512]{2,1,0:T(8,128)(2,1)} custom-call(bf16[2,2,64,512]{3,2,1,0:T(8,128)(2,1)} %bitcast.13, bf16[2048,4096]{1,0:T(8,128)(2,1)} %coulomb.1, bf16[1024,256]{1,0:T(8,128)(2,1)} %fusion.8.chosen), custom_call_target="tpu_custom_call" | custom-call | tf_op jit(solution)/shard_map/pallas_call | solution.py:317
  131.5 4.9 %shard_map.75 = f32[1024,512]{1,0:T(8,128)} custom-call(bf16[1024,1024]{1,0:T(8,128)(2,1)} %interp.1, bf16[1024,512]{1,0:T(8,128)(2,1)} %bitcast.12), custom_call_target="tpu_custom_call" | custom-call | tf_op jit(solution)/shard_map/pallas_call | solution.py:355
